TPU v7x, 32 devices: a whole 2x2x4 slice. The times are simulated.
32 devices in a mesh: tile: 8 (over z, x), section: 4 (over y, core).
Axes of the slice: x: 2, y: 2, z: 4, core: 2. Of those that a mesh axis runs over, the one named last changes fastest.
Arguments:
- states: bfloat16 [2, 192, 8, 8, 256], P(None, 'tile'), may hold values from -6 to 6
- conv_weight: bfloat16 [4, 2, 3, 3, 256, 256], P('section'), may hold values from -0.1875 to 0.1875
- skip_weight: bfloat16 [4, 256, 256], P('section'), may hold values from -0.375 to 0.375
- bias: bfloat16 [4, 2, 256], P('section'), may hold values from -3 to 3
- placement: int32 [8], replicated, may hold values from 0 to 7, each once
Outputs:
- activations: bfloat16 [4, 2, 192, 8, 8, 256], P('section', None, 'tile')
Inputs may be any that keep to these rules, and one draw needn't show every extreme that they name: placement is a permutation of 0 .. 7.
All inputs are finite; a program needn't handle non-finite values.
Results may differ from a plain program's by a relative error of at most 0.017.
Values may be sent and summed in bfloat16 or wider, within the bound.
A program may use at most 64 MiB of HBM per device.

v0:
```python
import jax
import jax.numpy as jnp
import numpy as np
from jax import lax
from jax.sharding import PartitionSpec as P

LAYERS = 2
PR = 4


def from_behind(x, axis, by):
    devices = lax.axis_size(axis)
    pairs = [(i, i + by) for i in range(devices) if 0 <= i + by < devices]
    return lax.ppermute(x, axis, pairs)


def face_across(face_num, direction):
    cycle = face_num // 4
    column = face_num % 4
    if cycle == 0:
        table = [4 + column, 4 + (column + 1) % 4, (column + 1) % 4, (column + 3) % 4]
    elif cycle == 1:
        table = [8 + (column + 3) % 4, 8 + column, column, (column + 3) % 4]
    else:
        table = [8 + (column + 3) % 4, 8 + (column + 1) % 4, 4 + (column + 1) % 4, 4 + column]
    return table[direction]


def locate(face_num, coord_x, coord_y, face_span):
    if 0 <= coord_x < face_span and 0 <= coord_y < face_span:
        return (face_num, coord_x, coord_y)
    if coord_x < 0:
        direction = 0
    elif coord_y < 0:
        direction = 1
    elif coord_x >= face_span:
        direction = 2
    else:
        direction = 3
    cycle = face_num // 4
    target = face_across(face_num, direction)
    coord_x = coord_x % face_span
    coord_y = coord_y % face_span
    if cycle == 0 and direction == 2 or (cycle == 2 and direction == 0):
        coord_x, coord_y = (coord_y, face_span - 1 - coord_x)
    elif cycle == 0 and direction == 3 or (cycle == 2 and direction == 1):
        coord_x, coord_y = (face_span - 1 - coord_y, coord_x)
    return (target, coord_x, coord_y)


def seam_tables(tiles):
    cell_side = 2
    face_span = tiles * cell_side
    face_tiles = tiles * tiles
    total = 12 * face_tiles
    neighbour = np.zeros((total, 4), np.int32)
    rim_side = np.zeros((total, 4), np.int32)
    flip_flag = np.zeros((total, 4), np.int32)
    for patch_num in range(total):
        cycle = patch_num % 3
        rest = patch_num // 3
        column = rest // face_tiles
        tile_y = rest % face_tiles // tiles
        tile_x = rest % tiles
        face_num = 4 * cycle + column
        base_x = tile_x * cell_side
        base_y = tile_y * cell_side
        for side_num in range(4):
            found = []
            for step_num in range(2):
                if side_num == 0:
                    point = (base_x - 1, base_y + step_num)
                elif side_num == 1:
                    point = (base_x + cell_side, base_y + step_num)
                elif side_num == 2:
                    point = (base_x + step_num, base_y - 1)
                else:
                    point = (base_x + step_num, base_y + cell_side)
                found.append(locate(face_num, point[0], point[1], face_span))
            face_a, first_x, first_y = found[0]
            face_b, second_x, second_y = found[1]
            neighbour[patch_num, side_num] = (
                3 * (face_a % 4 * face_tiles + first_y // cell_side * tiles + first_x // cell_side)
                + face_a // 4
            )
            if first_x == second_x:
                rim_side[patch_num, side_num] = 0 if first_x % cell_side == 0 else 1
                flip_flag[patch_num, side_num] = 1 if second_y < first_y else 0
            else:
                rim_side[patch_num, side_num] = 2 if first_y % cell_side == 0 else 3
                flip_flag[patch_num, side_num] = 1 if second_x < first_x else 0
    return (neighbour, rim_side, flip_flag)


def route_tables(neighbour, rim_side, flip_flag, tile_count, per_dev):
    source_dev = (neighbour // per_dev).reshape(-1)
    dest_dev = np.repeat(np.arange(neighbour.shape[0]) // per_dev, 4)
    keys = source_dev * tile_count + dest_dev
    order = np.argsort(keys, kind="stable")
    sorted_keys = keys[order]
    starts = np.searchsorted(sorted_keys, sorted_keys, side="left")
    slot_num = np.zeros(keys.shape[0], np.int64)
    slot_num[order] = np.arange(keys.shape[0]) - starts
    slot_count = int(slot_num.max()) + 1
    send_row = np.zeros((tile_count, tile_count, slot_count), np.int32)
    send_flip = np.zeros((tile_count, tile_count, slot_count), np.int32)
    send_row[source_dev, dest_dev, slot_num] = (neighbour % per_dev * 4 + rim_side).reshape(-1)
    send_flip[source_dev, dest_dev, slot_num] = flip_flag.reshape(-1)
    recv_dev = source_dev.reshape(tile_count, per_dev, 4).astype(np.int32)
    recv_slot = slot_num.reshape(tile_count, per_dev, 4).astype(np.int32)
    return (send_row, send_flip, recv_dev, recv_slot)


def on_device(states, conv_weight, skip_weight, bias, placement):
    section_count = lax.axis_size("section")
    section_id = lax.axis_index("section")
    half_sections = section_count // 2
    tile_count = lax.axis_size("tile")
    device = lax.axis_index("tile")
    micro_count = states.shape[0]
    per_dev = states.shape[1]
    tile_side = states.shape[2]
    channels = states.shape[4]
    conv_w = conv_weight[0]
    skip_w = skip_weight[0]
    biases = bias[0].astype(jnp.float32)
    my_block = placement[device]
    owner = (
        jnp.zeros((tile_count,), jnp.int32)
        .at[placement]
        .set(jnp.arange(tile_count, dtype=jnp.int32))
    )
    neighbour, rim_side, flip_flag = seam_tables(PR)
    send_row, send_flip, recv_dev, recv_slot = route_tables(
        neighbour, rim_side, flip_flag, tile_count, per_dev
    )
    send_rows = jnp.asarray(send_row)[my_block][placement]
    send_flips = jnp.asarray(send_flip)[my_block][placement]
    from_dev = owner[jnp.asarray(recv_dev)[my_block]]
    from_slot = jnp.asarray(recv_slot)[my_block]
    block_shape = (micro_count, per_dev, tile_side, tile_side, channels)
    saved_acts = jnp.zeros(block_shape, jnp.bfloat16)
    skip_buffer = jnp.zeros(block_shape, jnp.bfloat16)
    chain_in = jnp.zeros(block_shape[1:], jnp.bfloat16)
    tick_count = micro_count + section_count - 1
    for tick_num in range(tick_count):
        mb_index = tick_num - section_id
        is_live = (mb_index >= 0) & (mb_index < micro_count)
        mb_slot = jnp.clip(mb_index, 0, micro_count - 1)
        window_in = lax.dynamic_index_in_dim(states, mb_slot, 0, keepdims=False)
        inputs = jnp.where(section_id == 0, window_in, chain_in)
        stored_skip = lax.dynamic_index_in_dim(skip_buffer, mb_slot, 0, keepdims=False)
        skip_in = jnp.where(section_id < half_sections, window_in, stored_skip)
        run_hidden = inputs
        for layer_num in range(LAYERS):
            kernel = conv_w[layer_num]
            rim_stack = jnp.stack(
                [run_hidden[:, :, 0], run_hidden[:, :, -1], run_hidden[:, 0], run_hidden[:, -1]],
                axis=1,
            )
            flat_rims = rim_stack.reshape(per_dev * 4, tile_side, channels)
            outgoing = flat_rims[send_rows]
            outgoing = jnp.where(
                (send_flips == 1)[:, :, None, None], outgoing[:, :, ::-1], outgoing
            )
            received = lax.all_to_all(outgoing, "tile", split_axis=0, concat_axis=0, tiled=True)
            strips = received[from_dev, from_slot]
            corner = jnp.zeros((per_dev, 1, channels), jnp.bfloat16)
            middle = jnp.concatenate(
                [strips[:, 0][:, :, None], run_hidden, strips[:, 1][:, :, None]], axis=2
            )
            upper_row = jnp.concatenate([corner, strips[:, 2], corner], axis=1)[:, None]
            lower_row = jnp.concatenate([corner, strips[:, 3], corner], axis=1)[:, None]
            summed = lax.conv_general_dilated(
                jnp.concatenate([upper_row, middle, lower_row], axis=1),
                kernel,
                (1, 1),
                "VALID",
                dimension_numbers=("NHWC", "HWIO", "NHWC"),
                preferred_element_type=jnp.float32,
            )
            if layer_num == 0:
                projected = jnp.dot(
                    skip_in.reshape(per_dev * tile_side * tile_side, channels),
                    skip_w,
                    preferred_element_type=jnp.float32,
                )
                summed = summed + projected.reshape(per_dev, tile_side, tile_side, channels)
            run_hidden = jax.nn.gelu(summed + biases[layer_num], approximate=False).astype(
                jnp.bfloat16
            )
        saved_acts = jnp.where(
            is_live, lax.dynamic_update_index_in_dim(saved_acts, run_hidden, mb_slot, 0), saved_acts
        )
        if tick_num < tick_count - 1:
            chain_in = from_behind(run_hidden, "section", 1)
        if tick_num < micro_count + half_sections - 1:
            arrived = from_behind(run_hidden, "section", half_sections)
            skip_index = tick_num - section_id + half_sections
            keep_skip = (
                (section_id >= half_sections) & (skip_index >= 0) & (skip_index < micro_count)
            )
            skip_slot = jnp.clip(skip_index, 0, micro_count - 1)
            skip_buffer = jnp.where(
                keep_skip,
                lax.dynamic_update_index_in_dim(skip_buffer, arrived, skip_slot, 0),
                skip_buffer,
            )
    return saved_acts[None]


def solution(mesh):
    in_specs = (
        P(None, "tile", None, None, None),
        P("section", None, None, None, None, None),
        P("section", None, None),
        P("section", None, None),
        P(),
    )
    out_specs = P("section", None, "tile", None, None, None)
    return jax.shard_map(
        on_device, mesh=mesh, in_specs=in_specs, out_specs=out_specs, check_vma=False
    )
```

profile of v0, /device:TPU:1, one launch (start us, length us, event | category | flops | bytes accessed | tf_op | source)
XLA Modules:
  0.0 756.1 jit_solution(15196806511829836806)
XLA Ops:
  0.0 3.8 constant_dynamic-slice_fusion
  18.9 6.4 all-to-all-start
  29.1 43.3 %all-to-all-done = bf16[8,64,8,256]{3,2,1,0:T(8,128)(2,1)S(1)} async-done(((bf16[8,64,8,256]{3,2,1,0:T(8,128)(2,1)}), bf16[8,64,8,256]{3,2,1,0:T(8,128)(2,1)S(1)}, u32[]{:S(2)}, u32[]{:S(2)}) %all-to-all-start) | async-done | bytes 2097184 | tf_op jit(solution)/shard_map/all_to_all | solution.py:166
  77.9 4.2 fusion.2
  91.2 5.1 all-to-all-start.1
  96.3 47.5 %all-to-all-done.1 = bf16[8,64,8,256]{3,2,1,0:T(8,128)(2,1)S(1)} async-done(((bf16[8,64,8,256]{3,2,1,0:T(8,128)(2,1)}), bf16[8,64,8,256]{3,2,1,0:T(8,128)(2,1)S(1)}, u32[]{:S(2)}, u32[]{:S(2)}) %all-to-all-start.1) | async-done | bytes 2097184 | tf_op jit(solution)/shard_map/all_to_all | solution.py:166
  146.7 5.3 bitcast_dynamic-update-slice_fusion.1
  152.0 4.7 collective-permute-start
  156.7 8.9 %collective-permute-done = bf16[24,8,8,256]{3,0,2,1:T(8,128)(2,1)S(1)} collective-permute-done((bf16[24,8,8,256]{3,0,2,1:T(8,128)(2,1)S(1)}, bf16[24,8,8,256]{3,0,2,1:T(8,128)(2,1)S(1)}, u32[]{:S(2)}, u32[]{:S(2)}) %collective-permute-start) | collective-permute-done | bytes 786464 | tf_op jit(solution)/shard_map/ppermute | solution.py:14
  168.7 3.5 rev.32
  175.3 4.5 all-to-all-start.2
  181.3 13.3 %collective-permute-done.1 = bf16[24,8,8,256]{3,0,2,1:T(8,128)(2,1)S(1)} collective-permute-done((bf16[24,8,8,256]{3,0,2,1:T(8,128)(2,1)S(1)}, bf16[24,8,8,256]{3,0,2,1:T(8,128)(2,1)S(1)}, u32[]{:S(2)}, u32[]{:S(2)}) %collective-permute-start.1) | collective-permute-done | bytes 786464 | tf_op jit(solution)/shard_map/ppermute | solution.py:14
  195.0 25.5 %all-to-all-done.2 = bf16[8,64,8,256]{3,2,1,0:T(8,128)(2,1)} async-done(((bf16[8,64,8,256]{3,2,1,0:T(8,128)(2,1)}), bf16[8,64,8,256]{3,2,1,0:T(8,128)(2,1)}, u32[]{:S(2)}, u32[]{:S(2)}) %all-to-all-start.2) | async-done | bytes 2097184 | tf_op jit(solution)/shard_map/all_to_all | solution.py:166
  223.3 3.6 fusion.120
  226.9 4.3 fusion.8
  233.8 3.5 rev.33
  240.4 4.6 all-to-all-start.3
  245.0 46.3 %all-to-all-done.3 = bf16[8,64,8,256]{3,2,1,0:T(8,128)(2,1)} async-done(((bf16[8,64,8,256]{3,2,1,0:T(8,128)(2,1)}), bf16[8,64,8,256]{3,2,1,0:T(8,128)(2,1)}, u32[]{:S(2)}, u32[]{:S(2)}) %all-to-all-start.3) | async-done | bytes 2097184 | tf_op jit(solution)/shard_map/all_to_all | solution.py:166
  295.0 6.8 fusion.228
  303.9 8.9 %collective-permute-done.2 = bf16[24,8,8,256]{3,0,2,1:T(8,128)(2,1)S(1)} collective-permute-done((bf16[24,8,8,256]{3,0,2,1:T(8,128)(2,1)S(1)}, bf16[24,8,8,256]{3,0,2,1:T(8,128)(2,1)S(1)}, u32[]{:S(2)}, u32[]{:S(2)}) %collective-permute-start.2) | collective-permute-done | bytes 786464 | tf_op jit(solution)/shard_map/ppermute | solution.py:14
  315.9 3.5 rev.34
  322.4 4.5 all-to-all-start.4
  328.7 13.4 %collective-permute-done.3 = bf16[24,8,8,256]{3,0,2,1:T(8,128)(2,1)S(1)} collective-permute-done((bf16[24,8,8,256]{3,0,2,1:T(8,128)(2,1)}, bf16[24,8,8,256]{3,0,2,1:T(8,128)(2,1)S(1)}, u32[]{:S(2)}, u32[]{:S(2)}) %collective-permute-start.3) | collective-permute-done | bytes 786464 | tf_op jit(solution)/shard_map/ppermute | solution.py:14
  342.4 27.4 %all-to-all-done.4 = bf16[8,64,8,256]{3,2,1,0:T(8,128)(2,1)} async-done(((bf16[8,64,8,256]{3,2,1,0:T(8,128)(2,1)}), bf16[8,64,8,256]{3,2,1,0:T(8,128)(2,1)}, u32[]{:S(2)}, u32[]{:S(2)}) %all-to-all-start.4) | async-done | bytes 2097184 | tf_op jit(solution)/shard_map/all_to_all | solution.py:166
  372.6 3.6 fusion.139
  376.2 4.3 fusion.14
  383.2 3.5 rev.35
  389.7 4.5 all-to-all-start.5
  394.2 48.4 %all-to-all-done.5 = bf16[8,64,8,256]{3,2,1,0:T(8,128)(2,1)} async-done(((bf16[8,64,8,256]{3,2,1,0:T(8,128)(2,1)}), bf16[8,64,8,256]{3,2,1,0:T(8,128)(2,1)}, u32[]{:S(2)}, u32[]{:S(2)}) %all-to-all-start.5) | async-done | bytes 2097184 | tf_op jit(solution)/shard_map/all_to_all | solution.py:166
  446.4 6.8 fusion.225
  455.1 8.9 %collective-permute-done.4 = bf16[24,8,8,256]{3,0,2,1:T(8,128)(2,1)S(1)} collective-permute-done((bf16[24,8,8,256]{3,0,2,1:T(8,128)(2,1)S(1)}, bf16[24,8,8,256]{3,0,2,1:T(8,128)(2,1)S(1)}, u32[]{:S(2)}, u32[]{:S(2)}) %collective-permute-start.4) | collective-permute-done | bytes 786464 | tf_op jit(solution)/shard_map/ppermute | solution.py:14
  467.3 3.5 rev.36
  473.9 4.5 all-to-all-start.6
  479.9 13.7 %collective-permute-done.5 = bf16[24,8,8,256]{3,0,2,1:T(8,128)(2,1)S(1)} collective-permute-done((bf16[24,8,8,256]{3,0,2,1:T(8,128)(2,1)}, bf16[24,8,8,256]{3,0,2,1:T(8,128)(2,1)S(1)}, u32[]{:S(2)}, u32[]{:S(2)}) %collective-permute-start.5) | collective-permute-done | bytes 786464 | tf_op jit(solution)/shard_map/ppermute | solution.py:14
  493.9 27.4 %all-to-all-done.6 = bf16[8,64,8,256]{3,2,1,0:T(8,128)(2,1)} async-done(((bf16[8,64,8,256]{3,2,1,0:T(8,128)(2,1)}), bf16[8,64,8,256]{3,2,1,0:T(8,128)(2,1)}, u32[]{:S(2)}, u32[]{:S(2)}) %all-to-all-start.6) | async-done | bytes 2097184 | tf_op jit(solution)/shard_map/all_to_all | solution.py:166
  529.3 4.3 fusion.20
  536.4 3.5 rev.37
  542.9 4.6 all-to-all-start.7
  547.6 48.5 %all-to-all-done.7 = bf16[8,64,8,256]{3,2,1,0:T(8,128)(2,1)} async-done(((bf16[8,64,8,256]{3,2,1,0:T(8,128)(2,1)}), bf16[8,64,8,256]{3,2,1,0:T(8,128)(2,1)}, u32[]{:S(2)}, u32[]{:S(2)}) %all-to-all-start.7) | async-done | bytes 2097184 | tf_op jit(solution)/shard_map/all_to_all | solution.py:166
  598.9 7.1 fusion.222
  607.9 8.9 %collective-permute-done.6 = bf16[24,8,8,256]{3,0,2,1:T(8,128)(2,1)S(1)} collective-permute-done((bf16[24,8,8,256]{3,0,2,1:T(8,128)(2,1)S(1)}, bf16[24,8,8,256]{3,0,2,1:T(8,128)(2,1)S(1)}, u32[]{:S(2)}, u32[]{:S(2)}) %collective-permute-start.6) | collective-permute-done | bytes 786464 | tf_op jit(solution)/shard_map/ppermute | solution.py:14
  625.6 46.0 %all_to_all.50 = bf16[8,64,8,256]{3,2,1,0:T(8,128)(2,1)S(1)} all-to-all(bf16[8,64,8,256]{3,2,1,0:T(8,128)(2,1)S(1)} %broadcast_select_fusion.1), channel_id=1, replica_groups=mesh['tile'=8,'section'=4] {'tile'}, dimensions={0} | all-to-all | bytes 4194304 | tf_op jit(solution)/shard_map/all_to_all | solution.py:166
  677.2 4.3 fusion.26
  684.1 3.5 rev.39
  690.7 5.0 all-to-all-start.9
  695.8 47.2 %all-to-all-done.9 = bf16[8,64,8,256]{3,2,1,0:T(8,128)(2,1)} async-done(((bf16[8,64,8,256]{3,2,1,0:T(8,128)(2,1)}), bf16[8,64,8,256]{3,2,1,0:T(8,128)(2,1)}, u32[]{:S(2)}, u32[]{:S(2)}) %all-to-all-start.9) | async-done | bytes 2097184 | tf_op jit(solution)/shard_map/all_to_all | solution.py:166
  743.0 3.5 gather_fusion.22
  747.8 6.6 fusion.216
  (268 shorter events, 127.6 us)
Async XLA Ops:
  0.0 77.9 %copy-start = (bf16[1,256,256]{2,1,0:T(8,128)(2,1)S(1)}, bf16[1,256,256]{2,1,0:T(8,128)(2,1)}, u32[]{:S(2)}) copy-start(bf16[1,256,256]{2,1,0:T(8,128)(2,1)} %param.11) | copy-start | bytes 393220
  3.8 2.3 copy-start.45
  18.9 53.5 %all-to-all-start = ((bf16[8,64,8,256]{3,2,1,0:T(8,128)(2,1)}), bf16[8,64,8,256]{3,2,1,0:T(8,128)(2,1)S(1)}, u32[]{:S(2)}, u32[]{:S(2)}) async-start(bf16[8,64,8,256]{3,2,1,0:T(8,128)(2,1)} %broadcast_select_fusion.9), calls=%async_computation | async-start | bytes 4194304 | tf_op jit(solution)/shard_map/all_to_all | solution.py:166
  26.7 2.3 copy-start.39
  73.4 1.1 copy-start.29
  74.5 3.4 copy-start.21
  91.2 52.7 %all-to-all-start.1 = ((bf16[8,64,8,256]{3,2,1,0:T(8,128)(2,1)}), bf16[8,64,8,256]{3,2,1,0:T(8,128)(2,1)S(1)}, u32[]{:S(2)}, u32[]{:S(2)}) async-start(bf16[8,64,8,256]{3,2,1,0:T(8,128)(2,1)} %broadcast_select_fusion.8), calls=%async_computation.1 | async-start | bytes 4194304 | tf_op jit(solution)/shard_map/all_to_all | solution.py:166
  144.9 1.7 copy-start.40
  144.9 1.8 copy-start.33
  146.7 18.9 %copy-start.18 = (bf16[1,24,8,8,256]{4,3,2,1,0:T(8,128)(2,1)S(1)}, bf16[1,24,8,8,256]{4,3,2,1,0:T(8,128)(2,1)}, u32[]{:S(2)}) copy-start(bf16[1,24,8,8,256]{4,3,2,1,0:T(8,128)(2,1)} %get-tuple-element.8) | copy-start | bytes 2359300
  152.0 14.1 %copy-start.1 = (bf16[2,24,8,8,256]{4,1,3,2,0:T(8,128)(2,1)}, bf16[2,24,8,8,256]{4,1,3,2,0:T(8,128)(2,1)S(1)}, u32[]{:S(2)}) copy-start(bf16[2,24,8,8,256]{4,1,3,2,0:T(8,128)(2,1)S(1)} %get-tuple-element.112) | copy-start | bytes 4718596
  152.0 14.1 %copy-start.42 = (bf16[24,8,8,256]{3,0,2,1:T(8,128)(2,1)}, bf16[24,8,8,256]{3,0,2,1:T(8,128)(2,1)S(1)}, u32[]{:S(2)}) copy-start(bf16[24,8,8,256]{3,0,2,1:T(8,128)(2,1)S(1)} %get-tuple-element.113) | copy-start | bytes 2359300
  152.0 13.6 %collective-permute-start = (bf16[24,8,8,256]{3,0,2,1:T(8,128)(2,1)S(1)}, bf16[24,8,8,256]{3,0,2,1:T(8,128)(2,1)S(1)}, u32[]{:S(2)}, u32[]{:S(2)}) collective-permute-start(bf16[24,8,8,256]{3,0,2,1:T(8,128)(2,1)S(1)} %get-tuple-element.113), channel_id=1, source_target_pairs={{0,1},{1,2},{2,3},{4,5},{5,6},{6,7},{8,9},{9,10},{10,11},{12,13},{... | collective-permute-start | bytes 2359304 | tf_op jit(solution)/shard_map/ppermute | solution.py:14
  175.3 4.5 copy-start.43
  175.3 45.2 %all-to-all-start.2 = ((bf16[8,64,8,256]{3,2,1,0:T(8,128)(2,1)}), bf16[8,64,8,256]{3,2,1,0:T(8,128)(2,1)}, u32[]{:S(2)}, u32[]{:S(2)}) async-start(bf16[8,64,8,256]{3,2,1,0:T(8,128)(2,1)} %broadcast_select_fusion.7), calls=%async_computation.2 | async-start | bytes 4194304 | tf_op jit(solution)/shard_map/all_to_all | solution.py:166
  179.8 14.9 %collective-permute-start.1 = (bf16[24,8,8,256]{3,0,2,1:T(8,128)(2,1)S(1)}, bf16[24,8,8,256]{3,0,2,1:T(8,128)(2,1)S(1)}, u32[]{:S(2)}, u32[]{:S(2)}) collective-permute-start(bf16[24,8,8,256]{3,0,2,1:T(8,128)(2,1)S(1)} %copy-done.43), channel_id=1, source_target_pairs={{0,2},{1,3},{4,6},{5,7},{8,10},{9,11},{12,14},{13,15},{16,18},{17,... | collective-permute-start | bytes 2359304 | tf_op jit(solution)/shard_map/ppermute | solution.py:14
  195.0 31.9 %copy-start.9 = (bf16[2,24,8,8,256]{4,1,3,2,0:T(8,128)(2,1)}, bf16[2,24,8,8,256]{4,1,3,2,0:T(8,128)(2,1)S(1)}, u32[]{:S(2)}) copy-start(bf16[2,24,8,8,256]{4,1,3,2,0:T(8,128)(2,1)S(1)} %bitcast_dynamic-update-slice_fusion) | copy-start | bytes 4718596
  223.3 3.7 copy-start.19
  240.4 50.9 %all-to-all-start.3 = ((bf16[8,64,8,256]{3,2,1,0:T(8,128)(2,1)}), bf16[8,64,8,256]{3,2,1,0:T(8,128)(2,1)}, u32[]{:S(2)}, u32[]{:S(2)}) async-start(bf16[8,64,8,256]{3,2,1,0:T(8,128)(2,1)} %broadcast_select_fusion.6), calls=%async_computation.3 | async-start | bytes 4194304 | tf_op jit(solution)/shard_map/all_to_all | solution.py:166
  245.0 49.2 %copy-start.2 = (bf16[2,24,8,8,256]{4,1,3,2,0:T(8,128)(2,1)S(1)}, bf16[2,24,8,8,256]{4,1,3,2,0:T(8,128)(2,1)}, u32[]{:S(2)}) copy-start(bf16[2,24,8,8,256]{4,1,3,2,0:T(8,128)(2,1)} %copy-done.1) | copy-start | bytes 4718596
  295.0 17.7 %copy-start.16 = (bf16[1,24,8,8,256]{4,3,2,1,0:T(8,128)(2,1)S(1)}, bf16[1,24,8,8,256]{4,3,2,1,0:T(8,128)(2,1)}, u32[]{:S(2)}) copy-start(bf16[1,24,8,8,256]{4,3,2,1,0:T(8,128)(2,1)} %get-tuple-element.7) | copy-start | bytes 2359300
  301.9 11.4 %copy-start.3 = (bf16[2,24,8,8,256]{4,1,3,2,0:T(8,128)(2,1)}, bf16[2,24,8,8,256]{4,1,3,2,0:T(8,128)(2,1)S(1)}, u32[]{:S(2)}) copy-start(bf16[2,24,8,8,256]{4,1,3,2,0:T(8,128)(2,1)S(1)} %get-tuple-element.114) | copy-start | bytes 4718596
  301.9 11.4 %copy-start.44 = (bf16[24,8,8,256]{3,0,2,1:T(8,128)(2,1)}, bf16[24,8,8,256]{3,0,2,1:T(8,128)(2,1)S(1)}, u32[]{:S(2)}) copy-start(bf16[24,8,8,256]{3,0,2,1:T(8,128)(2,1)S(1)} %get-tuple-element.115) | copy-start | bytes 2359300
  301.9 10.9 %collective-permute-start.2 = (bf16[24,8,8,256]{3,0,2,1:T(8,128)(2,1)S(1)}, bf16[24,8,8,256]{3,0,2,1:T(8,128)(2,1)S(1)}, u32[]{:S(2)}, u32[]{:S(2)}) collective-permute-start(bf16[24,8,8,256]{3,0,2,1:T(8,128)(2,1)S(1)} %get-tuple-element.115), channel_id=1, source_target_pairs={{0,1},{1,2},{2,3},{4,5},{5,6},{6,7},{8,9},{9,10},{10,11},{12,13},{... | collective-permute-start | bytes 2359304 | tf_op jit(solution)/shard_map/ppermute | solution.py:14
  322.4 19.7 %copy-start.10 = (bf16[2,24,8,8,256]{4,1,3,2,0:T(8,128)(2,1)S(1)}, bf16[2,24,8,8,256]{4,1,3,2,0:T(8,128)(2,1)}, u32[]{:S(2)}) copy-start(bf16[2,24,8,8,256]{4,1,3,2,0:T(8,128)(2,1)} %copy-done.9) | copy-start | bytes 4718596
  322.4 47.3 %all-to-all-start.4 = ((bf16[8,64,8,256]{3,2,1,0:T(8,128)(2,1)}), bf16[8,64,8,256]{3,2,1,0:T(8,128)(2,1)}, u32[]{:S(2)}, u32[]{:S(2)}) async-start(bf16[8,64,8,256]{3,2,1,0:T(8,128)(2,1)} %broadcast_select_fusion.5), calls=%async_computation.4 | async-start | bytes 4194304 | tf_op jit(solution)/shard_map/all_to_all | solution.py:166
  326.9 15.2 %collective-permute-start.3 = (bf16[24,8,8,256]{3,0,2,1:T(8,128)(2,1)}, bf16[24,8,8,256]{3,0,2,1:T(8,128)(2,1)S(1)}, u32[]{:S(2)}, u32[]{:S(2)}) collective-permute-start(bf16[24,8,8,256]{3,0,2,1:T(8,128)(2,1)} %copy-done.44), channel_id=1, source_target_pairs={{0,2},{1,3},{4,6},{5,7},{8,10},{9,11},{12,14},{13,15},{16,18},{17,... | collective-permute-start | bytes 2359304 | tf_op jit(solution)/shard_map/ppermute | solution.py:14
  342.4 33.8 %copy-start.11 = (bf16[2,24,8,8,256]{4,1,3,2,0:T(8,128)(2,1)}, bf16[2,24,8,8,256]{4,1,3,2,0:T(8,128)(2,1)S(1)}, u32[]{:S(2)}) copy-start(bf16[2,24,8,8,256]{4,1,3,2,0:T(8,128)(2,1)S(1)} %fusion.227) | copy-start | bytes 4718596
  372.6 3.7 copy-start.17
  389.7 53.0 %all-to-all-start.5 = ((bf16[8,64,8,256]{3,2,1,0:T(8,128)(2,1)}), bf16[8,64,8,256]{3,2,1,0:T(8,128)(2,1)}, u32[]{:S(2)}, u32[]{:S(2)}) async-start(bf16[8,64,8,256]{3,2,1,0:T(8,128)(2,1)} %broadcast_select_fusion.4), calls=%async_computation.5 | async-start | bytes 4194304 | tf_op jit(solution)/shard_map/all_to_all | solution.py:166
  394.2 51.3 %copy-start.4 = (bf16[2,24,8,8,256]{4,1,3,2,0:T(8,128)(2,1)S(1)}, bf16[2,24,8,8,256]{4,1,3,2,0:T(8,128)(2,1)}, u32[]{:S(2)}) copy-start(bf16[2,24,8,8,256]{4,1,3,2,0:T(8,128)(2,1)} %copy-done.3) | copy-start | bytes 4718596
  453.2 11.4 %copy-start.5 = (bf16[2,24,8,8,256]{4,1,3,2,0:T(8,128)(2,1)}, bf16[2,24,8,8,256]{4,1,3,2,0:T(8,128)(2,1)S(1)}, u32[]{:S(2)}) copy-start(bf16[2,24,8,8,256]{4,1,3,2,0:T(8,128)(2,1)S(1)} %get-tuple-element.116) | copy-start | bytes 4718596
  453.2 11.4 %copy-start.41 = (bf16[24,8,8,256]{3,0,2,1:T(8,128)(2,1)}, bf16[24,8,8,256]{3,0,2,1:T(8,128)(2,1)S(1)}, u32[]{:S(2)}) copy-start(bf16[24,8,8,256]{3,0,2,1:T(8,128)(2,1)S(1)} %get-tuple-element.117) | copy-start | bytes 2359300
  453.2 10.8 %collective-permute-start.4 = (bf16[24,8,8,256]{3,0,2,1:T(8,128)(2,1)S(1)}, bf16[24,8,8,256]{3,0,2,1:T(8,128)(2,1)S(1)}, u32[]{:S(2)}, u32[]{:S(2)}) collective-permute-start(bf16[24,8,8,256]{3,0,2,1:T(8,128)(2,1)S(1)} %get-tuple-element.117), channel_id=1, source_target_pairs={{0,1},{1,2},{2,3},{4,5},{5,6},{6,7},{8,9},{9,10},{10,11},{12,13},{... | collective-permute-start | bytes 2359304 | tf_op jit(solution)/shard_map/ppermute | solution.py:14
  473.9 19.7 %copy-start.12 = (bf16[2,24,8,8,256]{4,1,3,2,0:T(8,128)(2,1)S(1)}, bf16[2,24,8,8,256]{4,1,3,2,0:T(8,128)(2,1)}, u32[]{:S(2)}) copy-start(bf16[2,24,8,8,256]{4,1,3,2,0:T(8,128)(2,1)} %copy-done.11) | copy-start | bytes 4718596
  473.9 47.4 %all-to-all-start.6 = ((bf16[8,64,8,256]{3,2,1,0:T(8,128)(2,1)}), bf16[8,64,8,256]{3,2,1,0:T(8,128)(2,1)}, u32[]{:S(2)}, u32[]{:S(2)}) async-start(bf16[8,64,8,256]{3,2,1,0:T(8,128)(2,1)} %broadcast_select_fusion.3), calls=%async_computation.6 | async-start | bytes 4194304 | tf_op jit(solution)/shard_map/all_to_all | solution.py:166
  478.4 15.2 %collective-permute-start.5 = (bf16[24,8,8,256]{3,0,2,1:T(8,128)(2,1)}, bf16[24,8,8,256]{3,0,2,1:T(8,128)(2,1)S(1)}, u32[]{:S(2)}, u32[]{:S(2)}) collective-permute-start(bf16[24,8,8,256]{3,0,2,1:T(8,128)(2,1)} %copy-done.41), channel_id=1, source_target_pairs={{0,2},{1,3},{4,6},{5,7},{8,10},{9,11},{12,14},{13,15},{16,18},{17,... | collective-permute-start | bytes 2359304 | tf_op jit(solution)/shard_map/ppermute | solution.py:14
  493.8 35.5 %copy-start.13 = (bf16[2,24,8,8,256]{4,1,3,2,0:T(8,128)(2,1)}, bf16[2,24,8,8,256]{4,1,3,2,0:T(8,128)(2,1)S(1)}, u32[]{:S(2)}) copy-start(bf16[2,24,8,8,256]{4,1,3,2,0:T(8,128)(2,1)S(1)} %fusion.224) | copy-start | bytes 4718596
  493.8 32.1 %copy-start.24 = (bf16[24,8,8,256]{3,0,2,1:T(8,128)(2,1)S(1)}, bf16[24,8,8,256]{3,0,2,1:T(8,128)(2,1)}, u32[]{:S(2)}) copy-start(bf16[24,8,8,256]{3,0,2,1:T(8,128)(2,1)} %copy-done.23) | copy-start | bytes 2359300
  542.9 53.1 %all-to-all-start.7 = ((bf16[8,64,8,256]{3,2,1,0:T(8,128)(2,1)}), bf16[8,64,8,256]{3,2,1,0:T(8,128)(2,1)}, u32[]{:S(2)}, u32[]{:S(2)}) async-start(bf16[8,64,8,256]{3,2,1,0:T(8,128)(2,1)} %broadcast_select_fusion.2), calls=%async_computation.7 | async-start | bytes 4194304 | tf_op jit(solution)/shard_map/all_to_all | solution.py:166
  547.5 51.3 %copy-start.6 = (bf16[2,24,8,8,256]{4,1,3,2,0:T(8,128)(2,1)S(1)}, bf16[2,24,8,8,256]{4,1,3,2,0:T(8,128)(2,1)}, u32[]{:S(2)}) copy-start(bf16[2,24,8,8,256]{4,1,3,2,0:T(8,128)(2,1)} %copy-done.5) | copy-start | bytes 4718596
  598.8 18.0 %copy-start.15 = (bf16[1,24,8,8,256]{4,3,2,1,0:T(8,128)(2,1)S(1)}, bf16[1,24,8,8,256]{4,3,2,1,0:T(8,128)(2,1)}, u32[]{:S(2)}) copy-start(bf16[1,24,8,8,256]{4,3,2,1,0:T(8,128)(2,1)} %get-tuple-element.5) | copy-start | bytes 2359300
  605.9 11.4 %copy-start.7 = (bf16[2,24,8,8,256]{4,1,3,2,0:T(8,128)(2,1)}, bf16[2,24,8,8,256]{4,1,3,2,0:T(8,128)(2,1)S(1)}, u32[]{:S(2)}) copy-start(bf16[2,24,8,8,256]{4,1,3,2,0:T(8,128)(2,1)S(1)} %get-tuple-element.118) | copy-start | bytes 4718596
  606.0 10.8 %collective-permute-start.6 = (bf16[24,8,8,256]{3,0,2,1:T(8,128)(2,1)S(1)}, bf16[24,8,8,256]{3,0,2,1:T(8,128)(2,1)S(1)}, u32[]{:S(2)}, u32[]{:S(2)}) collective-permute-start(bf16[24,8,8,256]{3,0,2,1:T(8,128)(2,1)S(1)} %get-tuple-element.119), channel_id=1, source_target_pairs={{0,1},{1,2},{2,3},{4,5},{5,6},{6,7},{8,9},{9,10},{10,11},{12,13},{... | collective-permute-start | bytes 2359304 | tf_op jit(solution)/shard_map/ppermute | solution.py:14
  673.8 3.4 copy-start.14
  690.7 5.0 copy-start.8
  690.7 52.4 %all-to-all-start.9 = ((bf16[8,64,8,256]{3,2,1,0:T(8,128)(2,1)}), bf16[8,64,8,256]{3,2,1,0:T(8,128)(2,1)}, u32[]{:S(2)}, u32[]{:S(2)}) async-start(bf16[8,64,8,256]{3,2,1,0:T(8,128)(2,1)} %broadcast_select_fusion), calls=%async_computation.9 | async-start | bytes 4194304 | tf_op jit(solution)/shard_map/all_to_all | solution.py:166
  746.5 1.3 copy-start.31
  (14 other events, 13.3 us)
where the time goes:
time: 765 us; the launch traced here: 756 us
  waiting for transfers between devices  438 us (57%)
  local copies, waits for them, and re-layouts  104 us (14%)
  matrix products  71.1 us (9%)
  starting transfers between devices  58.9 us (8%)
  blocking collectives  46 us (6%)
  other arithmetic  34.7 us (5%)
    all_to_all x9, waiting for transfers between devices, on_device(): lax.all_to_all(outgoing, 'tile', split_axis=0, concat_axis=0, tiled=True)  362 us
    ppermute x7, waiting for transfers between devices, from_behind(): return lax.ppermute(x, axis, pairs)  76 us
    conv_general_dilated x10, matrix products, on_device(): lax.conv_general_dilated(jnp.concatenate([upper_row, middle, lower_row],...  49.9 us
    all_to_all x1, blocking collectives, on_device(): lax.all_to_all(outgoing, 'tile', split_axis=0, concat_axis=0, tiled=True)  46 us
    all_to_all x9, starting transfers between devices, on_device(): lax.all_to_all(outgoing, 'tile', split_axis=0, concat_axis=0, tiled=True)  43.6 us
    rev x10, local copies, waits for them, and re-layouts, on_device(): outgoing[:, :, ::-1]  34.9 us
    select_n x10, other arithmetic, on_device(): jnp.where((send_flips == 1)[:, :, None, None], outgoing[:, :, ::-1], outg...  29.5 us
    gather x10, local copies, waits for them, and re-layouts, on_device(): strips = received[from_dev, from_slot]  22.9 us
  transfers between devices with their start and end apart: 16, of which 16 were waited for; matrix products, arithmetic and copies ran while one was open for 1% of the time, Pallas kernels for 0%

commit v1 on v0

v1 whole, which is shorter than its diff:
```python
import functools

import jax
import jax.numpy as jnp
import numpy as np
from jax import lax
from jax.experimental import pallas as pl
from jax.experimental.pallas import tpu as pltpu
from jax.sharding import PartitionSpec as P

LAYERS = 2
PR = 4


def face_across(face_num, direction):
    cycle = face_num // 4
    column = face_num % 4
    if cycle == 0:
        table = [4 + column, 4 + (column + 1) % 4, (column + 1) % 4, (column + 3) % 4]
    elif cycle == 1:
        table = [8 + (column + 3) % 4, 8 + column, column, (column + 3) % 4]
    else:
        table = [8 + (column + 3) % 4, 8 + (column + 1) % 4, 4 + (column + 1) % 4, 4 + column]
    return table[direction]


def locate(face_num, coord_x, coord_y, face_span):
    if 0 <= coord_x < face_span and 0 <= coord_y < face_span:
        return (face_num, coord_x, coord_y)
    if coord_x < 0:
        direction = 0
    elif coord_y < 0:
        direction = 1
    elif coord_x >= face_span:
        direction = 2
    else:
        direction = 3
    cycle = face_num // 4
    target = face_across(face_num, direction)
    coord_x = coord_x % face_span
    coord_y = coord_y % face_span
    if cycle == 0 and direction == 2 or (cycle == 2 and direction == 0):
        coord_x, coord_y = (coord_y, face_span - 1 - coord_x)
    elif cycle == 0 and direction == 3 or (cycle == 2 and direction == 1):
        coord_x, coord_y = (face_span - 1 - coord_y, coord_x)
    return (target, coord_x, coord_y)


def seam_tables(tiles):
    cell_side = 2
    face_span = tiles * cell_side
    face_tiles = tiles * tiles
    total = 12 * face_tiles
    neighbour = np.zeros((total, 4), np.int32)
    rim_side = np.zeros((total, 4), np.int32)
    flip_flag = np.zeros((total, 4), np.int32)
    for patch_num in range(total):
        cycle = patch_num % 3
        rest = patch_num // 3
        column = rest // face_tiles
        tile_y = rest % face_tiles // tiles
        tile_x = rest % tiles
        face_num = 4 * cycle + column
        base_x = tile_x * cell_side
        base_y = tile_y * cell_side
        for side_num in range(4):
            found = []
            for step_num in range(2):
                if side_num == 0:
                    point = (base_x - 1, base_y + step_num)
                elif side_num == 1:
                    point = (base_x + cell_side, base_y + step_num)
                elif side_num == 2:
                    point = (base_x + step_num, base_y - 1)
                else:
                    point = (base_x + step_num, base_y + cell_side)
                found.append(locate(face_num, point[0], point[1], face_span))
            face_a, first_x, first_y = found[0]
            face_b, second_x, second_y = found[1]
            neighbour[patch_num, side_num] = (
                3 * (face_a % 4 * face_tiles + first_y // cell_side * tiles + first_x // cell_side)
                + face_a // 4
            )
            if first_x == second_x:
                rim_side[patch_num, side_num] = 0 if first_x % cell_side == 0 else 1
                flip_flag[patch_num, side_num] = 1 if second_y < first_y else 0
            else:
                rim_side[patch_num, side_num] = 2 if first_y % cell_side == 0 else 3
                flip_flag[patch_num, side_num] = 1 if second_x < first_x else 0
    return (neighbour, rim_side, flip_flag)


def off_device_routes(neighbour, rim_side, flip_flag, tile_count, per_dev):
    source_dev = (neighbour // per_dev).reshape(-1)
    dest_dev = np.repeat(np.arange(neighbour.shape[0]) // per_dev, 4)
    row = (neighbour % per_dev * 4 + rim_side).reshape(-1)
    away = source_dev != dest_dev
    slot_num = np.zeros(row.shape[0], np.int64)
    counts = np.zeros((tile_count, tile_count), np.int64)
    for e in np.flatnonzero(away):
        slot_num[e] = counts[source_dev[e], dest_dev[e]]
        counts[source_dev[e], dest_dev[e]] += 1
    send_row = np.zeros((tile_count, tile_count, int(counts.max())), np.int32)
    send_row[source_dev[away], dest_dev[away], slot_num[away]] = row[away]
    place = np.where(away, slot_num, row)
    recv_dev = source_dev.reshape(tile_count, per_dev, 4).astype(np.int32)
    recv_slot = place.reshape(tile_count, per_dev, 4).astype(np.int32)
    return (send_row, None, recv_dev, recv_slot)


MESH = pl.DeviceIdType.MESH
LANES = 128


def joined(ref, span):
    return jnp.concatenate([ref[b, span, :] for b in range(ref.shape[0])], axis=1)


def split_store(ref, span, value):
    for b in range(ref.shape[0]):
        ref[b, span, :] = value[:, b * LANES:(b + 1) * LANES]


def window_kernel(
    tiles, sections, patches, micro, slots,
    send_rows, recv_self, recv_from, recv_row,
    states, weights, skip_w, biases,
    out,
    chain_in, skip_in, hidden, left, right, padded, edge_low, edge_high, rims,
    outgoing, received_a, received_b,
    halo_send, halo_recv, move_send, move_recv,
):
    tile = lax.axis_index("tile")
    section = lax.axis_index("section")
    half = sections // 2
    side = states.shape[1]
    rows = states.shape[2]
    chan = states.shape[3]
    received = (received_a, received_b)

    def tile_at(by):
        return lax.rem(tile + by, tiles)

    barrier = pltpu.get_barrier_semaphore()
    for by in range(1, tiles):
        pl.semaphore_signal(barrier, inc=1, device_id={"tile": tile_at(by)}, device_id_type=MESH)
    for by in range(1, sections):
        pl.semaphore_signal(
            barrier, inc=1, device_id={"section": lax.rem(section + by, sections)}, device_id_type=MESH
        )
    pl.semaphore_wait(barrier, tiles - 1 + sections - 1)

    @pl.when(section == 0)
    def _():
        chain_in[...] = states[...]

    @pl.when(section < half)
    def _():
        skip_in[...] = states[...]

    column = lax.broadcasted_iota(jnp.int32, (rows // 8, 8, chan), 1)
    first = column == 0
    last = column == 7

    def halo_copy(layer, by):
        return pltpu.make_async_remote_copy(
            src_ref=outgoing.at[layer, by - 1],
            dst_ref=received[layer].at[by - 1],
            send_sem=halo_send.at[layer, by - 1],
            recv_sem=halo_recv.at[layer, by - 1],
            device_id={"tile": tile_at(by)},
            device_id_type=MESH,
        )

    def chain_copy(m):
        return pltpu.make_async_remote_copy(
            src_ref=out.at[m], dst_ref=chain_in.at[m],
            send_sem=move_send.at[0, m], recv_sem=move_recv.at[0, m],
            device_id={"section": lax.rem(section + 1, sections)}, device_id_type=MESH,
        )

    def skip_copy(m):
        return pltpu.make_async_remote_copy(
            src_ref=out.at[m], dst_ref=skip_in.at[m],
            send_sem=move_send.at[1, m], recv_sem=move_recv.at[1, m],
            device_id={"section": lax.rem(section + half, sections)}, device_id_type=MESH,
        )

    def run_layer(m, layer):
        for p in range(patches):
            top = (side - 1) * rows + p * 8
            for b in range(chan // LANES):
                lanes = slice(b * LANES, (b + 1) * LANES)
                rims[4 * p, :, lanes] = hidden[b, pl.ds(p * 8, 8, stride=rows), :]
                rims[4 * p + 1, :, lanes] = hidden[b, pl.ds(p * 8 + 7, 8, stride=rows), :]
                rims[4 * p + 2, :, lanes] = hidden[b, p * 8:p * 8 + 8, :]
                rims[4 * p + 3, :, lanes] = hidden[b, top:top + 8, :]
        for by in range(1, tiles):
            for q in range(slots):
                outgoing[layer, by - 1, q] = rims[send_rows[by * slots + q]].astype(jnp.bfloat16)
            halo_copy(layer, by).start()
        for r in range(side):
            padded[r + 1, :, chan:2 * chan] = joined(hidden, slice(r * rows, (r + 1) * rows)).astype(jnp.bfloat16)
        for by in range(1, tiles):
            halo_copy(layer, by).wait_recv()
        for p in range(patches):
            for k in range(4):
                e = 4 * p + k
                strip = jnp.where(
                    recv_self[e] == 1,
                    rims[recv_row[e]],
                    received[layer][recv_from[e], lax.rem(recv_row[e], slots)].astype(jnp.float32),
                )
                if k == 0:
                    for b in range(chan // LANES):
                        left[b, pl.ds(p * 8, 8, stride=rows), :] = strip[:, b * LANES:(b + 1) * LANES]
                elif k == 1:
                    for b in range(chan // LANES):
                        right[b, pl.ds(p * 8 + 7, 8, stride=rows), :] = strip[:, b * LANES:(b + 1) * LANES]
                elif k == 2:
                    edge_low[p * 8:p * 8 + 8, :] = strip
                else:
                    edge_high[p * 8:p * 8 + 8, :] = strip
        for r in range(side + 2):
            if r == 0 or r == side + 1:
                values = (edge_low if r == 0 else edge_high)[...].reshape(rows // 8, 8, chan)
                before = jnp.zeros_like(values)
                after = before
                padded[r, :, chan:2 * chan] = values.reshape(rows, chan).astype(jnp.bfloat16)
            else:
                span = slice((r - 1) * rows, r * rows)
                values = joined(hidden, span).reshape(rows // 8, 8, chan)
                before = joined(left, span).reshape(rows // 8, 8, chan)
                after = joined(right, span).reshape(rows // 8, 8, chan)
            lower = jnp.where(first, before, pltpu.roll(values, 1, 1))
            upper = jnp.where(last, after, pltpu.roll(values, 7, 1))
            padded[r, :, 0:chan] = lower.reshape(rows, chan).astype(jnp.bfloat16)
            padded[r, :, 2 * chan:3 * chan] = upper.reshape(rows, chan).astype(jnp.bfloat16)

        step = 2

        @pl.loop(0, side // step)
        def _(part):
            r = part * step
            total = jnp.broadcast_to(biases[layer:layer + 1, :], (step * rows, chan))
            for i in range(3):
                total += jnp.dot(
                    padded[pl.ds(r + i, step)].reshape(step * rows, 3 * chan),
                    weights[layer, i],
                    preferred_element_type=jnp.float32,
                )
            if layer == 0:
                total += jnp.dot(
                    skip_in[m, pl.ds(r, step)].reshape(step * rows, chan),
                    skip_w[...],
                    preferred_element_type=jnp.float32,
                )
            value = 0.5 * total * (1.0 + lax.erf(total * np.float32(0.5 ** 0.5)))
            if layer == LAYERS - 1:
                out[m, pl.ds(r, step)] = value.reshape(step, rows, chan).astype(jnp.bfloat16)
            else:
                split_store(hidden, pl.ds(pl.multiple_of(r * rows, 8), step * rows), value)

        for by in range(1, tiles):
            halo_copy(layer, by).wait_send()

    @pl.loop(0, micro)
    def _(m):
        @pl.when(section > 0)
        def _():
            chain_copy(m).wait_recv()

        @pl.when(section >= half)
        def _():
            skip_copy(m).wait_recv()

        for r in range(side):
            split_store(hidden, slice(r * rows, (r + 1) * rows), chain_in[m, r].astype(jnp.float32))
        for layer in range(LAYERS):
            run_layer(m, layer)

        @pl.when(section < sections - 1)
        def _():
            chain_copy(m).start()

        @pl.when(section < sections - half)
        def _():
            skip_copy(m).start()

    @pl.loop(0, micro)
    def _(m):
        @pl.when(section < sections - 1)
        def _():
            chain_copy(m).wait_send()

        @pl.when(section < sections - half)
        def _():
            skip_copy(m).wait_send()


def on_device(states, conv_weight, skip_weight, bias, placement):
    sections = lax.axis_size("section")
    tiles = lax.axis_size("tile")
    device = lax.axis_index("tile")
    micro, patches, side, _, chan = states.shape
    neighbour, rim_side, flip_flag = seam_tables(PR)
    assert not flip_flag.any()
    send_row, _, recv_dev, recv_slot = off_device_routes(neighbour, rim_side, flip_flag, tiles, patches)
    slots = send_row.shape[2]
    whole = patches + patches % 2
    rows = whole * side
    my_block = placement[device]
    order = jnp.arange(tiles, dtype=jnp.int32)
    owner = jnp.zeros((tiles,), jnp.int32).at[placement].set(order)
    to_block = placement[(device + order) % tiles]
    send_rows = jnp.asarray(send_row)[my_block][to_block].reshape(-1)
    source = jnp.asarray(recv_dev)[my_block].reshape(-1)
    recv_self = (source == my_block).astype(jnp.int32)
    by = (device - owner[source] + tiles) % tiles
    recv_from = jnp.maximum(by - 1, 0).astype(jnp.int32)
    recv_row = jnp.asarray(recv_slot)[my_block].reshape(-1)

    ordered = states.transpose(0, 2, 1, 3, 4)
    if whole != patches:
        ordered = jnp.pad(ordered, ((0, 0), (0, 0), (0, whole - patches), (0, 0), (0, 0)))
    ordered = ordered.reshape(micro, side, rows, chan)
    weights = conv_weight[0].reshape(LAYERS, 3, 3 * chan, chan)
    smem = pl.BlockSpec(memory_space=pltpu.SMEM)
    vmem = pl.BlockSpec(memory_space=pltpu.VMEM)
    field = pltpu.VMEM((micro, side, rows, chan), jnp.bfloat16)
    wide = pltpu.VMEM((chan // LANES, side * rows, LANES), jnp.float32)
    edge = pltpu.VMEM((rows, chan), jnp.float32)
    got = pltpu.VMEM((tiles - 1, slots, side, chan), jnp.bfloat16)
    flops = 2 * micro * side * rows * chan * chan * (9 * LAYERS + 1)
    result = pl.pallas_call(
        functools.partial(window_kernel, tiles, sections, patches, micro, slots),
        out_shape=jax.ShapeDtypeStruct((micro, side, rows, chan), jnp.bfloat16),
        in_specs=[smem] * 4 + [vmem] * 4,
        out_specs=vmem,
        scratch_shapes=[
            field, field, wide, wide, wide,
            pltpu.VMEM((side + 2, rows, 3 * chan), jnp.bfloat16),
            edge, edge,
            pltpu.VMEM((patches * 4, side, chan), jnp.float32),
            pltpu.VMEM((2, tiles - 1, slots, side, chan), jnp.bfloat16),
            got, got,
            pltpu.SemaphoreType.DMA((2, tiles - 1)),
            pltpu.SemaphoreType.DMA((2, tiles - 1)),
            pltpu.SemaphoreType.DMA((2, micro)),
            pltpu.SemaphoreType.DMA((2, micro)),
        ],
        compiler_params=pltpu.CompilerParams(
            collective_id=0, has_side_effects=True, vmem_limit_bytes=56 * 1024 * 1024
        ),
        cost_estimate=pl.CostEstimate(flops=flops, bytes_accessed=2**24, transcendentals=0),
    )(
        send_rows, recv_self, recv_from, recv_row,
        ordered, weights, skip_weight[0], bias[0].astype(jnp.float32),
    )
    result = result.reshape(micro, side, whole, side, chan)[:, :, :patches]
    return result.transpose(0, 2, 1, 3, 4)[None]


def solution(mesh):
    in_specs = (
        P(None, "tile", None, None, None),
        P("section", None, None, None, None, None),
        P("section", None, None),
        P("section", None, None),
        P(),
    )
    out_specs = P("section", None, "tile", None, None, None)
    return jax.shard_map(
        on_device, mesh=mesh, in_specs=in_specs, out_specs=out_specs, check_vma=False
    )
```

time: 765 us -> 186 us (0.24)
  the two profiles are of different devices: /device:TPU:1 before, /device:TPU:13 now
where the time goes in v1:
time: 186 us
  Pallas kernels  163 us (88%)
  local copies, waits for them, and re-layouts  11.9 us (6%)
  other arithmetic  8.88 us (5%)
  between operations  1.99 us (1%)
    pallas_call x1, Pallas kernels, on_device(): pl.pallas_call(functools.partial(window_kernel, tiles, sections, patches,...  163 us
    max x1, other arithmetic, on_device(): recv_from = jnp.maximum(by - 1, 0).astype(jnp.int32)  5.59 us

profile of v1, /device:TPU:13, one launch (start us, length us, event | category | flops | bytes accessed | tf_op | source)
XLA Modules:
  0.0 185.8 jit_solution(17750193236062206319)
XLA Ops:
  0.0 0.0 copy-start
  0.0 1.4 dynamic_slice.12
  3.3 0.7 compare_select_fusion.1
  4.0 0.6 scatter_custom_fusion
  4.6 1.2 bitcast_convert_fusion.biases
  5.8 1.3 gather_fusion
  7.2 0.7 fusion.11
  7.8 0.7 dynamic-slice_bitcast_fusion
  8.5 0.6 gather_fusion.1
  9.1 0.7 reshape.105.send_rows
  9.7 1.4 compare_convert_fusion
  11.1 0.6 reshape.108.recv_self
  11.7 0.7 constant_dynamic-slice_fusion
  12.4 0.6 reshape_squeeze.10.recv_row
  13.0 0.1 reshape_squeeze.9
  13.1 5.6 %fusion.1.recv_from = s32[96]{0:T(128)} fusion(s32[96,1]{0,1:T(1,128)S(1)} %reshape_squeeze.9, s32[]{:T(128)} %bitcast.7, s32[]{:T(128)} %bitcast.8, s32[]{:T(128)} %bitcast.9, s32[]{:T(128)} %bitcast.10, s32[]{:T(128)} %bitcast.11, s32[]{:T(128)} %bitcast.13, s32[]{:T(128)} %bitcast.12, s32[]{:T(128)} %bitcast.6, s32[]{:T(128)S(6)} %axis_index.15), kind=kLoop, calls=%fused_computation.30 | loop fusion | flops 3072 | bytes 804 | tf_op jit(solution)/shard_map/max | solution.py:320
  18.7 0.0 copy-done
  18.7 1.3 copy_bitcast_fusion.1.states
  20.0 163.0 %shard_map.82 = bf16[2,8,192,256]{3,2,1,0:T(8,128)(2,1)} custom-call(s32[128]{0:T(128)} %reshape.105.send_rows, s32[96]{0:T(128)} %reshape.108.recv_self, s32[96]{0:T(128)} %fusion.1.recv_from, s32[96]{0:T(128)} %reshape_squeeze.10.recv_row, bf16[2,8,192,256]{3,2,1,0:T(8,128)(2,1)} %copy_bitcast_fusion.1.states, bf16[2,3,768,256]{3,2,1,0:T(8,128)(2,1)} %bitcast.57, ...), custom_call_target="tpu_custom_call" | custom-call | flops 7650410496 | bytes 16777216 | tf_op jit(solution)/shard_map/pallas_call | solution.py:335
  183.0 2.8 %copy_bitcast_fusion = bf16[1,2,24,8,8,256]{5,4,3,2,1,0:T(8,128)(2,1)} fusion(bf16[2,8,192,256]{3,2,1,0:T(8,128)(2,1)} %shard_map.82), kind=kLoop, calls=%fused_computation.3 | loop fusion | bytes 3145728 | tf_op jit(solution)/shard_map/broadcast_in_dim | solution.py:361
  (5 shorter events, 0.0 us)
Async XLA Ops:
  0.0 18.7 %copy-start = (bf16[2,24,8,8,256]{4,3,2,1,0:T(8,128)(2,1)S(1)}, bf16[2,24,8,8,256]{4,3,2,1,0:T(8,128)(2,1)}, u32[]{:S(2)}) copy-start(bf16[2,24,8,8,256]{4,3,2,1,0:T(8,128)(2,1)} %param.8) | copy-start | bytes 4718596

commit v2 on v1

--- a/solution.py
+++ b/solution.py
@@ -123,11 +123,11 @@
 
 def window_kernel(
     tiles, sections, patches, micro, slots,
-    send_rows, recv_self, recv_from, recv_row,
+    placement, table,
     states, weights, skip_w, biases,
     out,
-    chain_in, skip_in, hidden, left, right, padded, edge_low, edge_high, rims,
-    outgoing, received_a, received_b,
+    chain_in, skip_in, hidden, summed, padded, edges, rims,
+    outgoing, received_a, received_b, behind,
     halo_send, halo_recv, move_send, move_recv,
 ):
     tile = lax.axis_index("tile")
@@ -150,6 +150,22 @@
         )
     pl.semaphore_wait(barrier, tiles - 1 + sections - 1)
 
+    my_block = placement[tile]
+    sources = tiles * tiles * slots + my_block * (4 * patches)
+    places = sources + tiles * 4 * patches
+
+    @pl.loop(0, tiles)
+    def _(block):
+        def one(by, found):
+            here = placement[lax.rem(tile - by + tiles, tiles)]
+            return jnp.where(here == block, by, found)
+
+        behind[block] = lax.fori_loop(0, tiles, one, jnp.int32(0))
+
+    nothing = jnp.zeros((rows, 3 * chan), jnp.bfloat16)
+    padded[0] = nothing
+    padded[side + 1] = nothing
+
     @pl.when(section == 0)
     def _():
         chain_in[...] = states[...]
@@ -185,6 +201,15 @@
             send_sem=move_send.at[1, m], recv_sem=move_recv.at[1, m],
             device_id={"section": lax.rem(section + half, sections)}, device_id_type=MESH,
         )
+
+    def gelu(z):
+        return 0.5 * z * (1.0 + lax.erf(z * np.float32(0.5 ** 0.5)))
+
+    def shifted(values):
+        cells = values.reshape(rows // 8, 8, chan)
+        lower = jnp.where(first, 0.0, pltpu.roll(cells, 1, 1)).reshape(rows, chan)
+        upper = jnp.where(last, 0.0, pltpu.roll(cells, 7, 1)).reshape(rows, chan)
+        return jnp.concatenate([lower, values, upper], axis=1).astype(jnp.bfloat16)
 
     def run_layer(m, layer):
         for p in range(patches):
@@ -196,46 +221,14 @@
                 rims[4 * p + 2, :, lanes] = hidden[b, p * 8:p * 8 + 8, :]
                 rims[4 * p + 3, :, lanes] = hidden[b, top:top + 8, :]
         for by in range(1, tiles):
+            base = (my_block * tiles + placement[tile_at(by)]) * slots
             for q in range(slots):
-                outgoing[layer, by - 1, q] = rims[send_rows[by * slots + q]].astype(jnp.bfloat16)
+                outgoing[layer, by - 1, q] = rims[table[base + q]].astype(jnp.bfloat16)
             halo_copy(layer, by).start()
+
         for r in range(side):
-            padded[r + 1, :, chan:2 * chan] = joined(hidden, slice(r * rows, (r + 1) * rows)).astype(jnp.bfloat16)
-        for by in range(1, tiles):
-            halo_copy(layer, by).wait_recv()
-        for p in range(patches):
-            for k in range(4):
-                e = 4 * p + k
-                strip = jnp.where(
-                    recv_self[e] == 1,
-                    rims[recv_row[e]],
-                    received[layer][recv_from[e], lax.rem(recv_row[e], slots)].astype(jnp.float32),
-                )
-                if k == 0:
-                    for b in range(chan // LANES):
-                        left[b, pl.ds(p * 8, 8, stride=rows), :] = strip[:, b * LANES:(b + 1) * LANES]
-                elif k == 1:
-                    for b in range(chan // LANES):
-                        right[b, pl.ds(p * 8 + 7, 8, stride=rows), :] = strip[:, b * LANES:(b + 1) * LANES]
-                elif k == 2:
-                    edge_low[p * 8:p * 8 + 8, :] = strip
-                else:
-                    edge_high[p * 8:p * 8 + 8, :] = strip
-        for r in range(side + 2):
-            if r == 0 or r == side + 1:
-                values = (edge_low if r == 0 else edge_high)[...].reshape(rows // 8, 8, chan)
-                before = jnp.zeros_like(values)
-                after = before
-                padded[r, :, chan:2 * chan] = values.reshape(rows, chan).astype(jnp.bfloat16)
-            else:
-                span = slice((r - 1) * rows, r * rows)
-                values = joined(hidden, span).reshape(rows // 8, 8, chan)
-                before = joined(left, span).reshape(rows // 8, 8, chan)
-                after = joined(right, span).reshape(rows // 8, 8, chan)
-            lower = jnp.where(first, before, pltpu.roll(values, 1, 1))
-            upper = jnp.where(last, after, pltpu.roll(values, 7, 1))
-            padded[r, :, 0:chan] = lower.reshape(rows, chan).astype(jnp.bfloat16)
-            padded[r, :, 2 * chan:3 * chan] = upper.reshape(rows, chan).astype(jnp.bfloat16)
+            values = joined(hidden, slice(r * rows, (r + 1) * rows))
+            padded[r + 1] = shifted(values)
 
         step = 2
 
@@ -255,12 +248,46 @@
                     skip_w[...],
                     preferred_element_type=jnp.float32,
                 )
-            value = 0.5 * total * (1.0 + lax.erf(total * np.float32(0.5 ** 0.5)))
-            if layer == LAYERS - 1:
-                out[m, pl.ds(r, step)] = value.reshape(step, rows, chan).astype(jnp.bfloat16)
-            else:
-                split_store(hidden, pl.ds(pl.multiple_of(r * rows, 8), step * rows), value)
-
+            span = pl.ds(pl.multiple_of(r * rows, 8), step * rows)
+            split_store(summed, span, total)
+            split_store(hidden, span, gelu(total))
+
+        for by in range(1, tiles):
+            halo_copy(layer, by).wait_recv()
+        for e in range(4 * patches):
+            by = behind[table[sources + e]]
+            row = table[places + e]
+            edges[e % 4, e // 4 * 8:e // 4 * 8 + 8, :] = jnp.where(
+                by == 0,
+                rims[row],
+                received[layer][jnp.maximum(by - 1, 0), lax.rem(row, slots)].astype(jnp.float32),
+            )
+        for k in (2, 3):
+            row = 0 if k == 2 else side - 1
+            added = jnp.dot(
+                shifted(edges[k]), weights[layer, k * 2 - 4], preferred_element_type=jnp.float32
+            )
+            span = slice(row * rows, (row + 1) * rows)
+            total = joined(summed, span) + added
+            split_store(summed, span, total)
+            split_store(hidden, span, gelu(total))
+        for k in (0, 1):
+            moved = shifted(edges[k])
+            added = jnp.zeros((rows, chan), jnp.float32)
+            for i in range(3):
+                added += jnp.dot(
+                    moved[:, i * chan:(i + 1) * chan],
+                    weights[layer, i, k * 2 * chan:(k * 2 + 1) * chan],
+                    preferred_element_type=jnp.float32,
+                )
+            for p in range(patches):
+                span = pl.ds(p * 8 + k * 7, 8, stride=rows)
+                for b in range(chan // LANES):
+                    part = added[p * 8:p * 8 + 8, b * LANES:(b + 1) * LANES]
+                    hidden[b, span, :] = gelu(summed[b, span, :] + part)
+        if layer == LAYERS - 1:
+            for r in range(side):
+                out[m, r] = joined(hidden, slice(r * rows, (r + 1) * rows)).astype(jnp.bfloat16)
         for by in range(1, tiles):
             halo_copy(layer, by).wait_send()
 
@@ -301,7 +328,6 @@
 def on_device(states, conv_weight, skip_weight, bias, placement):
     sections = lax.axis_size("section")
     tiles = lax.axis_size("tile")
-    device = lax.axis_index("tile")
     micro, patches, side, _, chan = states.shape
     neighbour, rim_side, flip_flag = seam_tables(PR)
     assert not flip_flag.any()
@@ -309,17 +335,7 @@
     slots = send_row.shape[2]
     whole = patches + patches % 2
     rows = whole * side
-    my_block = placement[device]
-    order = jnp.arange(tiles, dtype=jnp.int32)
-    owner = jnp.zeros((tiles,), jnp.int32).at[placement].set(order)
-    to_block = placement[(device + order) % tiles]
-    send_rows = jnp.asarray(send_row)[my_block][to_block].reshape(-1)
-    source = jnp.asarray(recv_dev)[my_block].reshape(-1)
-    recv_self = (source == my_block).astype(jnp.int32)
-    by = (device - owner[source] + tiles) % tiles
-    recv_from = jnp.maximum(by - 1, 0).astype(jnp.int32)
-    recv_row = jnp.asarray(recv_slot)[my_block].reshape(-1)
-
+    table = np.concatenate([x.reshape(-1) for x in (send_row, recv_dev, recv_slot)])
     ordered = states.transpose(0, 2, 1, 3, 4)
     if whole != patches:
         ordered = jnp.pad(ordered, ((0, 0), (0, 0), (0, whole - patches), (0, 0), (0, 0)))
@@ -329,21 +345,21 @@
     vmem = pl.BlockSpec(memory_space=pltpu.VMEM)
     field = pltpu.VMEM((micro, side, rows, chan), jnp.bfloat16)
     wide = pltpu.VMEM((chan // LANES, side * rows, LANES), jnp.float32)
-    edge = pltpu.VMEM((rows, chan), jnp.float32)
     got = pltpu.VMEM((tiles - 1, slots, side, chan), jnp.bfloat16)
     flops = 2 * micro * side * rows * chan * chan * (9 * LAYERS + 1)
     result = pl.pallas_call(
         functools.partial(window_kernel, tiles, sections, patches, micro, slots),
         out_shape=jax.ShapeDtypeStruct((micro, side, rows, chan), jnp.bfloat16),
-        in_specs=[smem] * 4 + [vmem] * 4,
+        in_specs=[smem] * 2 + [vmem] * 4,
         out_specs=vmem,
         scratch_shapes=[
-            field, field, wide, wide, wide,
+            field, field, wide, wide,
             pltpu.VMEM((side + 2, rows, 3 * chan), jnp.bfloat16),
-            edge, edge,
+            pltpu.VMEM((4, rows, chan), jnp.float32),
             pltpu.VMEM((patches * 4, side, chan), jnp.float32),
             pltpu.VMEM((2, tiles - 1, slots, side, chan), jnp.bfloat16),
             got, got,
+            pltpu.SMEM((tiles,), jnp.int32),
             pltpu.SemaphoreType.DMA((2, tiles - 1)),
             pltpu.SemaphoreType.DMA((2, tiles - 1)),
             pltpu.SemaphoreType.DMA((2, micro)),
@@ -354,7 +370,7 @@
         ),
         cost_estimate=pl.CostEstimate(flops=flops, bytes_accessed=2**24, transcendentals=0),
     )(
-        send_rows, recv_self, recv_from, recv_row,
+        placement, jnp.asarray(table, jnp.int32),
         ordered, weights, skip_weight[0], bias[0].astype(jnp.float32),
     )
     result = result.reshape(micro, side, whole, side, chan)[:, :, :patches]

time: 186 us -> 145 us (0.78)
  Pallas kernels: 163 us -> 139 us
  local copies, waits for them, and re-layouts: 11.9 us -> 4.1 us
  other arithmetic: 8.88 us -> 1.38 us
  between operations: 1.99 us -> 0.01 us
    pallas_call x1, Pallas kernels: 163 us -> 139 us  [on_device(): pl.pallas_call(functools.partial(window_kernel, tiles, sections, patches,...]
    max x1 -> x0, other arithmetic: 5.59 us -> none  [on_device(): recv_from = jnp.maximum(by - 1, 0).astype(jnp.int32)]
    gather x3 -> x0, local copies, waits for them, and re-layouts: 2.53 us -> none  [the longest x1 1.29 us: on_device(): to_block = placement[(device + order) % tiles]]
    dynamic_slice x2 -> x0, local copies, waits for them, and re-layouts: 2.08 us -> none  [the longest x1 1.36 us: on_device(): my_block = placement[device]]
where the time goes in v2:
time: 145 us; the launch traced here: 144 us
  Pallas kernels  139 us (96%)
  local copies, waits for them, and re-layouts  4.1 us (3%)
    pallas_call x1, Pallas kernels, on_device(): pl.pallas_call(functools.partial(window_kernel, tiles, sections, patches,...  139 us

profile of v2, /device:TPU:13, one launch (start us, length us, event | category | flops | bytes accessed | tf_op | source)
XLA Modules:
  0.0 144.5 jit_solution(8324688607147563844)
XLA Ops:
  0.0 0.0 copy-start
  0.0 1.4 bitcast_convert_fusion.biases
  1.4 0.0 copy-done
  1.4 1.3 copy_bitcast_fusion.1.states
  2.7 139.0 %shard_map.64 = bf16[2,8,192,256]{3,2,1,0:T(8,128)(2,1)} custom-call(s32[8]{0:T(128)} %placement.1, s32[2560]{0:T(1024)} %constant.2.clone.table, bf16[2,8,192,256]{3,2,1,0:T(8,128)(2,1)} %copy_bitcast_fusion.1.states, bf16[2,3,768,256]{3,2,1,0:T(8,128)(2,1)} %bitcast.17, bf16[256,256]{1,0:T(8,128)(2,1)} %bitcast.18, f32[2,256]{1,0:T(2,128)} %bitcast_convert_fusion.biases), custom_call_target="tpu_custom_call" | custom-call | flops 7650410496 | bytes 16777216 | tf_op jit(solution)/shard_map/pallas_call | solution.py:350
  141.7 2.8 %copy_bitcast_fusion = bf16[1,2,24,8,8,256]{5,4,3,2,1,0:T(8,128)(2,1)} fusion(bf16[2,8,192,256]{3,2,1,0:T(8,128)(2,1)} %shard_map.64), kind=kLoop, calls=%fused_computation | loop fusion | bytes 3145728 | tf_op jit(solution)/shard_map/broadcast_in_dim | solution.py:377
Async XLA Ops:
  0.0 1.4 copy-start

commit v3 on v2

--- a/solution.py
+++ b/solution.py
@@ -126,9 +126,9 @@
     placement, table,
     states, weights, skip_w, biases,
     out,
-    chain_in, skip_in, hidden, summed, padded, edges, rims,
+    held, skip_held, bias_held, stage, hidden, summed, padded, edges, rims,
     outgoing, received_a, received_b, behind,
-    halo_send, halo_recv, move_send, move_recv,
+    halo_send, halo_recv, weight_send, weight_recv, own_sem, out_send, out_recv, ready,
 ):
     tile = lax.axis_index("tile")
     section = lax.axis_index("section")
@@ -150,6 +150,9 @@
         )
     pl.semaphore_wait(barrier, tiles - 1 + sections - 1)
 
+    group = sections // micro
+    works = lax.rem(section, group) == 0
+    mine = section // group
     my_block = placement[tile]
     sources = tiles * tiles * slots + my_block * (4 * patches)
     places = sources + tiles * 4 * patches
@@ -165,14 +168,6 @@
     nothing = jnp.zeros((rows, 3 * chan), jnp.bfloat16)
     padded[0] = nothing
     padded[side + 1] = nothing
-
-    @pl.when(section == 0)
-    def _():
-        chain_in[...] = states[...]
-
-    @pl.when(section < half)
-    def _():
-        skip_in[...] = states[...]
 
     column = lax.broadcasted_iota(jnp.int32, (rows // 8, 8, chan), 1)
     first = column == 0
@@ -188,19 +183,40 @@
             device_id_type=MESH,
         )
 
-    def chain_copy(m):
+    pieces = ((weights.at[0], held, 0), (weights.at[1], held, 1), (skip_w, skip_held, None), (biases, bias_held, None))
+
+    def weight_copy(piece, source, worker):
+        src, dst, layer = pieces[piece]
         return pltpu.make_async_remote_copy(
-            src_ref=out.at[m], dst_ref=chain_in.at[m],
-            send_sem=move_send.at[0, m], recv_sem=move_recv.at[0, m],
-            device_id={"section": lax.rem(section + 1, sections)}, device_id_type=MESH,
+            src_ref=src,
+            dst_ref=dst.at[source] if layer is None else dst.at[source, layer],
+            send_sem=weight_send.at[worker, piece],
+            recv_sem=weight_recv.at[source, piece],
+            device_id={"section": worker * group},
+            device_id_type=MESH,
         )
 
-    def skip_copy(m):
+    def own_copy(piece):
+        src, dst, layer = pieces[piece]
+        return pltpu.make_async_copy(
+            src, dst.at[section] if layer is None else dst.at[section, layer], own_sem.at[piece]
+        )
+
+    def out_copy(m, sec):
         return pltpu.make_async_remote_copy(
-            src_ref=out.at[m], dst_ref=skip_in.at[m],
-            send_sem=move_send.at[1, m], recv_sem=move_recv.at[1, m],
-            device_id={"section": lax.rem(section + half, sections)}, device_id_type=MESH,
+            src_ref=stage.at[half + sec], dst_ref=out.at[m],
+            send_sem=out_send.at[sec], recv_sem=out_recv.at[m],
+            device_id={"section": sec}, device_id_type=MESH,
         )
+
+    def need(piece, sec):
+        @pl.when(sec == section)
+        def _():
+            own_copy(piece).wait()
+
+        @pl.when(sec != section)
+        def _():
+            weight_copy(piece, sec, 0).wait_recv()
 
     def gelu(z):
         return 0.5 * z * (1.0 + lax.erf(z * np.float32(0.5 ** 0.5)))
@@ -211,7 +227,7 @@
         upper = jnp.where(last, 0.0, pltpu.roll(cells, 7, 1)).reshape(rows, chan)
         return jnp.concatenate([lower, values, upper], axis=1).astype(jnp.bfloat16)
 
-    def run_layer(m, layer):
+    def run_layer(sec, layer):
         for p in range(patches):
             top = (side - 1) * rows + p * 8
             for b in range(chan // LANES):
@@ -231,21 +247,34 @@
             padded[r + 1] = shifted(values)
 
         step = 2
+        if layer == 0:
+            need(3, sec)
+            need(2, sec)
+        need(layer, sec)
+        if layer == LAYERS - 1:
+            after = sec + 1
+
+            @pl.when((after < sections) & (lax.rem(after, group) > 0) & (after // group != mine))
+            def _():
+                pl.semaphore_signal(
+                    ready.at[mine], inc=1, device_id={"section": lax.rem(after, sections)},
+                    device_id_type=MESH,
+                )
 
         @pl.loop(0, side // step)
         def _(part):
             r = part * step
-            total = jnp.broadcast_to(biases[layer:layer + 1, :], (step * rows, chan))
+            total = jnp.broadcast_to(bias_held[sec, layer:layer + 1, :], (step * rows, chan))
             for i in range(3):
                 total += jnp.dot(
                     padded[pl.ds(r + i, step)].reshape(step * rows, 3 * chan),
-                    weights[layer, i],
+                    held[sec, layer, i],
                     preferred_element_type=jnp.float32,
                 )
             if layer == 0:
                 total += jnp.dot(
-                    skip_in[m, pl.ds(r, step)].reshape(step * rows, chan),
-                    skip_w[...],
+                    stage[sec, pl.ds(r, step)].reshape(step * rows, chan),
+                    skip_held[sec],
                     preferred_element_type=jnp.float32,
                 )
             span = pl.ds(pl.multiple_of(r * rows, 8), step * rows)
@@ -265,7 +294,7 @@
         for k in (2, 3):
             row = 0 if k == 2 else side - 1
             added = jnp.dot(
-                shifted(edges[k]), weights[layer, k * 2 - 4], preferred_element_type=jnp.float32
+                shifted(edges[k]), held[sec, layer, k * 2 - 4], preferred_element_type=jnp.float32
             )
             span = slice(row * rows, (row + 1) * rows)
             total = joined(summed, span) + added
@@ -277,7 +306,7 @@
             for i in range(3):
                 added += jnp.dot(
                     moved[:, i * chan:(i + 1) * chan],
-                    weights[layer, i, k * 2 * chan:(k * 2 + 1) * chan],
+                    held[sec, layer, i, k * 2 * chan:(k * 2 + 1) * chan],
                     preferred_element_type=jnp.float32,
                 )
             for p in range(patches):
@@ -287,42 +316,71 @@
                     hidden[b, span, :] = gelu(summed[b, span, :] + part)
         if layer == LAYERS - 1:
             for r in range(side):
-                out[m, r] = joined(hidden, slice(r * rows, (r + 1) * rows)).astype(jnp.bfloat16)
+                stage[half + sec, r] = joined(hidden, slice(r * rows, (r + 1) * rows)).astype(jnp.bfloat16)
         for by in range(1, tiles):
             halo_copy(layer, by).wait_send()
 
-    @pl.loop(0, micro)
-    def _(m):
-        @pl.when(section > 0)
-        def _():
-            chain_copy(m).wait_recv()
-
-        @pl.when(section >= half)
-        def _():
-            skip_copy(m).wait_recv()
-
+    def send_weights(worker, which):
+        for piece in which:
+            weight_copy(piece, section, worker).start()
+
+    @pl.when(works)
+    def _():
+        for piece in (3, 2, 0, 1):
+            own_copy(piece).start()
+
+    for worker in range(micro):
+        @pl.when((section != worker * group) & (works | (mine == worker)))
+        def _():
+            send_weights(worker, (3, 2, 0))
+
+        @pl.when((section != worker * group) & (mine == worker))
+        def _():
+            send_weights(worker, (1,))
+
+    for worker in range(micro):
+        @pl.when(jnp.logical_not(works) & (mine != worker))
+        def _():
+            pl.semaphore_wait(ready.at[worker], 1)
+            send_weights(worker, (3, 2, 0, 1))
+
+    @pl.when(works)
+    def _():
+        for i in range(half):
+            stage[i] = states[mine]
         for r in range(side):
-            split_store(hidden, slice(r * rows, (r + 1) * rows), chain_in[m, r].astype(jnp.float32))
-        for layer in range(LAYERS):
-            run_layer(m, layer)
-
-        @pl.when(section < sections - 1)
-        def _():
-            chain_copy(m).start()
-
-        @pl.when(section < sections - half)
-        def _():
-            skip_copy(m).start()
-
-    @pl.loop(0, micro)
-    def _(m):
-        @pl.when(section < sections - 1)
-        def _():
-            chain_copy(m).wait_send()
-
-        @pl.when(section < sections - half)
-        def _():
-            skip_copy(m).wait_send()
+            split_store(hidden, slice(r * rows, (r + 1) * rows), states[mine, r].astype(jnp.float32))
+
+        @pl.loop(0, sections)
+        def _(sec):
+            for layer in range(LAYERS):
+                run_layer(sec, layer)
+                if layer == 0:
+                    for worker in range(micro):
+                        @pl.when((sec == 0) & (worker != mine))
+                        def _():
+                            send_weights(worker, (1,))
+
+            @pl.when(sec == section)
+            def _():
+                out[mine] = stage[half + sec]
+
+            @pl.when(sec != section)
+            def _():
+                out_copy(mine, sec).start()
+
+        @pl.loop(0, sections)
+        def _(sec):
+            @pl.when(sec != section)
+            def _():
+                out_copy(mine, sec).wait_send()
+
+    for worker in range(micro):
+        @pl.when(section != worker * group)
+        def _():
+            for piece in range(4):
+                weight_copy(piece, section, worker).wait_send()
+            out_copy(worker, section).wait_recv()
 
 
 def on_device(states, conv_weight, skip_weight, bias, placement):
@@ -341,19 +399,24 @@
         ordered = jnp.pad(ordered, ((0, 0), (0, 0), (0, whole - patches), (0, 0), (0, 0)))
     ordered = ordered.reshape(micro, side, rows, chan)
     weights = conv_weight[0].reshape(LAYERS, 3, 3 * chan, chan)
+    biases = jnp.pad(bias[0].astype(jnp.float32), ((0, 8 - LAYERS), (0, 0)))
+    held = sections + sections // 2
     smem = pl.BlockSpec(memory_space=pltpu.SMEM)
     vmem = pl.BlockSpec(memory_space=pltpu.VMEM)
-    field = pltpu.VMEM((micro, side, rows, chan), jnp.bfloat16)
     wide = pltpu.VMEM((chan // LANES, side * rows, LANES), jnp.float32)
     got = pltpu.VMEM((tiles - 1, slots, side, chan), jnp.bfloat16)
     flops = 2 * micro * side * rows * chan * chan * (9 * LAYERS + 1)
     result = pl.pallas_call(
         functools.partial(window_kernel, tiles, sections, patches, micro, slots),
         out_shape=jax.ShapeDtypeStruct((micro, side, rows, chan), jnp.bfloat16),
-        in_specs=[smem] * 2 + [vmem] * 4,
+        in_specs=[smem] * 2 + [vmem, pl.BlockSpec(memory_space=pl.ANY), vmem, vmem],
         out_specs=vmem,
         scratch_shapes=[
-            field, field, wide, wide,
+            pltpu.VMEM((sections,) + weights.shape, jnp.bfloat16),
+            pltpu.VMEM((sections, chan, chan), jnp.bfloat16),
+            pltpu.VMEM((sections, 8, chan), jnp.float32),
+            pltpu.VMEM((held, side, rows, chan), jnp.bfloat16),
+            wide, wide,
             pltpu.VMEM((side + 2, rows, 3 * chan), jnp.bfloat16),
             pltpu.VMEM((4, rows, chan), jnp.float32),
             pltpu.VMEM((patches * 4, side, chan), jnp.float32),
@@ -362,8 +425,12 @@
             pltpu.SMEM((tiles,), jnp.int32),
             pltpu.SemaphoreType.DMA((2, tiles - 1)),
             pltpu.SemaphoreType.DMA((2, tiles - 1)),
-            pltpu.SemaphoreType.DMA((2, micro)),
-            pltpu.SemaphoreType.DMA((2, micro)),
+            pltpu.SemaphoreType.DMA((micro, 4)),
+            pltpu.SemaphoreType.DMA((sections, 4)),
+            pltpu.SemaphoreType.DMA((4,)),
+            pltpu.SemaphoreType.DMA((sections,)),
+            pltpu.SemaphoreType.DMA((micro,)),
+            pltpu.SemaphoreType.REGULAR((micro,)),
         ],
         compiler_params=pltpu.CompilerParams(
             collective_id=0, has_side_effects=True, vmem_limit_bytes=56 * 1024 * 1024
@@ -371,7 +438,7 @@
         cost_estimate=pl.CostEstimate(flops=flops, bytes_accessed=2**24, transcendentals=0),
     )(
         placement, jnp.asarray(table, jnp.int32),
-        ordered, weights, skip_weight[0], bias[0].astype(jnp.float32),
+        ordered, weights, skip_weight[0], biases,
     )
     result = result.reshape(micro, side, whole, side, chan)[:, :, :patches]
     return result.transpose(0, 2, 1, 3, 4)[None]

time: 145 us -> 116 us (0.80)
  Pallas kernels: 139 us -> 110 us
    pallas_call x1, Pallas kernels: 139 us -> 110 us  [on_device(): pl.pallas_call(functools.partial(window_kernel, tiles, sections, patches,...]
where the time goes in v3:
time: 116 us
  Pallas kernels  110 us (95%)
  local copies, waits for them, and re-layouts  4.08 us (4%)
  other arithmetic  1.4 us (1%)
    pallas_call x1, Pallas kernels, on_device(): pl.pallas_call(functools.partial(window_kernel, tiles, sections, patches,...  110 us
    broadcast_in_dim x1, local copies, waits for them, and re-layouts, on_device(): return result.transpose(0, 2, 1, 3, 4)[None]  2.76 us

profile of v3, /device:TPU:13, one launch (start us, length us, event | category | flops | bytes accessed | tf_op | source)
XLA Modules:
  0.0 115.9 jit_solution(17248103023948106308)
XLA Ops:
  0.0 0.0 copy-start
  0.0 1.4 %pad_convert_fusion.biases = f32[8,256]{1,0:T(8,128)} fusion(bf16[2,256]{1,0:T(2,128)(2,1)} %bitcast.15), kind=kLoop, calls=%fused_computation.2 | loop fusion | flops 2048 | bytes 9216 | tf_op jit(solution)/shard_map/jit(_pad)/pad | solution.py:402
  1.4 0.0 copy-done
  1.4 1.3 %copy_bitcast_fusion.1.states = bf16[2,8,192,256]{3,2,1,0:T(8,128)(2,1)} fusion(bf16[2,24,8,8,256]{4,3,2,1,0:T(8,128)(2,1)S(1)} %copy-done), kind=kLoop, calls=%fused_computation.1 | loop fusion | bytes 3145728 | tf_op jit(solution)/shard_map/reshape | solution.py:400
  2.7 110.4 %shard_map.64 = bf16[2,8,192,256]{3,2,1,0:T(8,128)(2,1)} custom-call(s32[8]{0:T(128)} %placement.1, s32[2560]{0:T(1024)} %constant.6.clone.table, bf16[2,8,192,256]{3,2,1,0:T(8,128)(2,1)} %copy_bitcast_fusion.1.states, bf16[2,3,768,256]{3,2,1,0:T(8,128)(2,1)} %bitcast.16, bf16[256,256]{1,0:T(8,128)(2,1)} %bitcast.17, f32[8,256]{1,0:T(8,128)} %pad_convert_fusion.biases), custom_call_target="tpu_custom_call" | custom-call | flops 7650410496 | bytes 16777216 | tf_op jit(solution)/shard_map/pallas_call | solution.py:409
  113.1 2.8 %copy_bitcast_fusion = bf16[1,2,24,8,8,256]{5,4,3,2,1,0:T(8,128)(2,1)} fusion(bf16[2,8,192,256]{3,2,1,0:T(8,128)(2,1)} %shard_map.64), kind=kLoop, calls=%fused_computation | loop fusion | bytes 3145728 | tf_op jit(solution)/shard_map/broadcast_in_dim | solution.py:444
Async XLA Ops:
  0.0 1.4 %copy-start = (bf16[2,24,8,8,256]{4,3,2,1,0:T(8,128)(2,1)S(1)}, bf16[2,24,8,8,256]{4,3,2,1,0:T(8,128)(2,1)}, u32[]{:S(2)}) copy-start(bf16[2,24,8,8,256]{4,3,2,1,0:T(8,128)(2,1)} %param.6) | copy-start | bytes 4718596

commit v4 on v3

--- a/solution.py
+++ b/solution.py
@@ -129,6 +129,7 @@
     held, skip_held, bias_held, stage, hidden, summed, padded, edges, rims,
     outgoing, received_a, received_b, behind,
     halo_send, halo_recv, weight_send, weight_recv, own_sem, out_send, out_recv, ready,
+    relay_send, relay_recv, pass_send, pass_recv,
 ):
     tile = lax.axis_index("tile")
     section = lax.axis_index("section")
@@ -141,6 +142,7 @@
     def tile_at(by):
         return lax.rem(tile + by, tiles)
 
+    partner = tile + 1 - 2 * lax.rem(tile, 2)
     barrier = pltpu.get_barrier_semaphore()
     for by in range(1, tiles):
         pl.semaphore_signal(barrier, inc=1, device_id={"tile": tile_at(by)}, device_id_type=MESH)
@@ -148,7 +150,11 @@
         pl.semaphore_signal(
             barrier, inc=1, device_id={"section": lax.rem(section + by, sections)}, device_id_type=MESH
         )
-    pl.semaphore_wait(barrier, tiles - 1 + sections - 1)
+        pl.semaphore_signal(
+            barrier, inc=1, device_id={"tile": partner, "section": lax.rem(section + by, sections)},
+            device_id_type=MESH,
+        )
+    pl.semaphore_wait(barrier, tiles - 1 + 2 * (sections - 1))
 
     group = sections // micro
     works = lax.rem(section, group) == 0
@@ -214,9 +220,41 @@
         def _():
             own_copy(piece).wait()
 
-        @pl.when(sec != section)
+        near = sec // group == mine
+
+        @pl.when((sec != section) & (near if piece < 2 else True))
         def _():
             weight_copy(piece, sec, 0).wait_recv()
+
+        if piece < 2:
+            @pl.when(jnp.logical_not(near))
+            def _():
+                for hop in range(2):
+                    pass_copy(piece, sec, hop, hop).wait_recv()
+
+    deep = 3 * chan // 2
+
+    def part(other):
+        which = lax.rem(tile + other, 2)
+        return pl.ds(pl.multiple_of(which * deep, LANES), deep)
+
+    def relay_copy(layer, source, worker):
+        return pltpu.make_async_remote_copy(
+            src_ref=weights.at[layer, :, part(0)], dst_ref=held.at[source, layer, :, part(0)],
+            send_sem=relay_send.at[worker, layer], recv_sem=relay_recv.at[source, layer],
+            device_id={"section": worker * group + 1}, device_id_type=MESH,
+        )
+
+    def pass_copy(layer, source, hop, other):
+        place = held.at[source, layer, :, part(other)]
+        device = {"section": mine * group}
+        if hop == 1:
+            device["tile"] = partner
+        return pltpu.make_async_remote_copy(
+            src_ref=place, dst_ref=place,
+            send_sem=pass_send.at[source, layer, hop], recv_sem=pass_recv.at[source, layer, hop],
+            device_id=device, device_id_type=MESH,
+        )
 
     def gelu(z):
         return 0.5 * z * (1.0 + lax.erf(z * np.float32(0.5 ** 0.5)))
@@ -251,16 +289,6 @@
             need(3, sec)
             need(2, sec)
         need(layer, sec)
-        if layer == LAYERS - 1:
-            after = sec + 1
-
-            @pl.when((after < sections) & (lax.rem(after, group) > 0) & (after // group != mine))
-            def _():
-                pl.semaphore_signal(
-                    ready.at[mine], inc=1, device_id={"section": lax.rem(after, sections)},
-                    device_id_type=MESH,
-                )
-
         @pl.loop(0, side // step)
         def _(part):
             r = part * step
@@ -330,19 +358,50 @@
             own_copy(piece).start()
 
     for worker in range(micro):
-        @pl.when((section != worker * group) & (works | (mine == worker)))
-        def _():
-            send_weights(worker, (3, 2, 0))
+        @pl.when(section != worker * group)
+        def _():
+            send_weights(worker, (3, 2))
 
         @pl.when((section != worker * group) & (mine == worker))
         def _():
-            send_weights(worker, (1,))
-
-    for worker in range(micro):
-        @pl.when(jnp.logical_not(works) & (mine != worker))
-        def _():
-            pl.semaphore_wait(ready.at[worker], 1)
-            send_weights(worker, (3, 2, 0, 1))
+            send_weights(worker, (0, 1))
+
+        @pl.when(works & (mine != worker))
+        def _():
+            for layer in range(LAYERS):
+                relay_copy(layer, section, worker).start()
+
+    relays = lax.rem(section, group) == 1
+
+    def pass_on(source):
+        for layer in range(LAYERS):
+            relay_copy(layer, source, 0).wait_recv()
+            for hop in range(2):
+                pass_copy(layer, source, hop, 0).start()
+
+    for rank in range(group):
+        for worker in range(micro):
+            source = worker * group + rank
+
+            @pl.when(relays & (mine != worker))
+            def _():
+                pass_on(source)
+
+        if rank + 1 < group:
+            for worker in range(micro):
+                @pl.when(relays & (mine != worker))
+                def _():
+                    pl.semaphore_signal(
+                        ready.at[mine], inc=1, device_id={"section": worker * group + rank + 1},
+                        device_id_type=MESH,
+                    )
+
+            for worker in range(micro):
+                @pl.when((lax.rem(section, group) == rank + 1) & (mine != worker))
+                def _():
+                    pl.semaphore_wait(ready.at[worker], 1)
+                    for layer in range(LAYERS):
+                        relay_copy(layer, section, worker).start()
 
     @pl.when(works)
     def _():
@@ -355,11 +414,6 @@
         def _(sec):
             for layer in range(LAYERS):
                 run_layer(sec, layer)
-                if layer == 0:
-                    for worker in range(micro):
-                        @pl.when((sec == 0) & (worker != mine))
-                        def _():
-                            send_weights(worker, (1,))
 
             @pl.when(sec == section)
             def _():
@@ -378,9 +432,26 @@
     for worker in range(micro):
         @pl.when(section != worker * group)
         def _():
-            for piece in range(4):
+            for piece in (2, 3):
                 weight_copy(piece, section, worker).wait_send()
             out_copy(worker, section).wait_recv()
+
+        @pl.when((section != worker * group) & (mine == worker))
+        def _():
+            for piece in (0, 1):
+                weight_copy(piece, section, worker).wait_send()
+
+        @pl.when(mine != worker)
+        def _():
+            for layer in range(LAYERS):
+                relay_copy(layer, section, worker).wait_send()
+
+        @pl.when(relays & (mine != worker))
+        def _():
+            for rank in range(group):
+                for layer in range(LAYERS):
+                    for hop in range(2):
+                        pass_copy(layer, worker * group + rank, hop, 0).wait_send()
 
 
 def on_device(states, conv_weight, skip_weight, bias, placement):
@@ -431,6 +502,10 @@
             pltpu.SemaphoreType.DMA((sections,)),
             pltpu.SemaphoreType.DMA((micro,)),
             pltpu.SemaphoreType.REGULAR((micro,)),
+            pltpu.SemaphoreType.DMA((micro, LAYERS)),
+            pltpu.SemaphoreType.DMA((sections, LAYERS)),
+            pltpu.SemaphoreType.DMA((sections, LAYERS, 2)),
+            pltpu.SemaphoreType.DMA((sections, LAYERS, 2)),
         ],
         compiler_params=pltpu.CompilerParams(
             collective_id=0, has_side_effects=True, vmem_limit_bytes=56 * 1024 * 1024

time: 116 us -> 105 us (0.905)
  Pallas kernels: 110 us -> 99.6 us
    pallas_call x1, Pallas kernels: 110 us -> 99.6 us  [on_device(): pl.pallas_call(functools.partial(window_kernel, tiles, sections, patches,...]
where the time goes in v4:
time: 105 us
  Pallas kernels  99.6 us (95%)
  local copies, waits for them, and re-layouts  4.08 us (4%)
  other arithmetic  1.4 us (1%)
    pallas_call x1, Pallas kernels, on_device(): pl.pallas_call(functools.partial(window_kernel, tiles, sections, patches,...  99.6 us
    broadcast_in_dim x1, local copies, waits for them, and re-layouts, on_device(): return result.transpose(0, 2, 1, 3, 4)[None]  2.76 us

profile of v4, /device:TPU:13, one launch (start us, length us, event | category | flops | bytes accessed | tf_op | source)
XLA Modules:
  0.0 105.1 jit_solution(10333578712813698003)
XLA Ops:
  0.0 0.0 copy-start
  0.0 1.4 %pad_convert_fusion.biases = f32[8,256]{1,0:T(8,128)} fusion(bf16[2,256]{1,0:T(2,128)(2,1)} %bitcast.15), kind=kLoop, calls=%fused_computation.2 | loop fusion | flops 2048 | bytes 9216 | tf_op jit(solution)/shard_map/jit(_pad)/pad | solution.py:473
  1.4 0.0 copy-done
  1.4 1.3 %copy_bitcast_fusion.1.states = bf16[2,8,192,256]{3,2,1,0:T(8,128)(2,1)} fusion(bf16[2,24,8,8,256]{4,3,2,1,0:T(8,128)(2,1)S(1)} %copy-done), kind=kLoop, calls=%fused_computation.1 | loop fusion | bytes 3145728 | tf_op jit(solution)/shard_map/reshape | solution.py:471
  2.7 99.6 %shard_map.64 = bf16[2,8,192,256]{3,2,1,0:T(8,128)(2,1)} custom-call(s32[8]{0:T(128)} %placement.1, s32[2560]{0:T(1024)} %constant.6.clone.table, bf16[2,8,192,256]{3,2,1,0:T(8,128)(2,1)} %copy_bitcast_fusion.1.states, bf16[2,3,768,256]{3,2,1,0:T(8,128)(2,1)} %bitcast.16, bf16[256,256]{1,0:T(8,128)(2,1)} %bitcast.17, f32[8,256]{1,0:T(8,128)} %pad_convert_fusion.biases), custom_call_target="tpu_custom_call" | custom-call | flops 7650410496 | bytes 16777216 | tf_op jit(solution)/shard_map/pallas_call | solution.py:480
  102.3 2.8 %copy_bitcast_fusion = bf16[1,2,24,8,8,256]{5,4,3,2,1,0:T(8,128)(2,1)} fusion(bf16[2,8,192,256]{3,2,1,0:T(8,128)(2,1)} %shard_map.64), kind=kLoop, calls=%fused_computation | loop fusion | bytes 3145728 | tf_op jit(solution)/shard_map/broadcast_in_dim | solution.py:519
Async XLA Ops:
  0.0 1.4 %copy-start = (bf16[2,24,8,8,256]{4,3,2,1,0:T(8,128)(2,1)S(1)}, bf16[2,24,8,8,256]{4,3,2,1,0:T(8,128)(2,1)}, u32[]{:S(2)}) copy-start(bf16[2,24,8,8,256]{4,3,2,1,0:T(8,128)(2,1)} %param.6) | copy-start | bytes 4718596

commit v5 on v4

--- a/solution.py
+++ b/solution.py
@@ -368,7 +368,13 @@
 
         @pl.when(works & (mine != worker))
         def _():
-            for layer in range(LAYERS):
+            relay_copy(0, section, worker).start()
+
+    for worker in range(micro):
+        @pl.when(works & (mine != worker))
+        def _():
+            for layer in range(1, LAYERS):
+                relay_copy(layer - 1, section, worker).wait_send()
                 relay_copy(layer, section, worker).start()
 
     relays = lax.rem(section, group) == 1
@@ -400,7 +406,9 @@
                 @pl.when((lax.rem(section, group) == rank + 1) & (mine != worker))
                 def _():
                     pl.semaphore_wait(ready.at[worker], 1)
-                    for layer in range(LAYERS):
+                    relay_copy(0, section, worker).start()
+                    for layer in range(1, LAYERS):
+                        relay_copy(layer - 1, section, worker).wait_send()
                         relay_copy(layer, section, worker).start()
 
     @pl.when(works)
@@ -443,8 +451,7 @@
 
         @pl.when(mine != worker)
         def _():
-            for layer in range(LAYERS):
-                relay_copy(layer, section, worker).wait_send()
+            relay_copy(LAYERS - 1, section, worker).wait_send()
 
         @pl.when(relays & (mine != worker))
         def _():

time: 105 us -> 111 us (1.057)
  Pallas kernels: 99.6 us -> 105 us
    pallas_call x1, Pallas kernels: 99.6 us -> 105 us  [on_device(): pl.pallas_call(functools.partial(window_kernel, tiles, sections, patches,...]
where the time goes in v5:
time: 111 us; the launch traced here: 110 us
  Pallas kernels  105 us (95%)
  local copies, waits for them, and re-layouts  4.08 us (4%)
  other arithmetic  1.4 us (1%)
    pallas_call x1, Pallas kernels, on_device(): pl.pallas_call(functools.partial(window_kernel, tiles, sections, patches,...  105 us
    broadcast_in_dim x1, local copies, waits for them, and re-layouts, on_device(): return result.transpose(0, 2, 1, 3, 4)[None]  2.76 us

profile of v5, /device:TPU:13, one launch (start us, length us, event | category | flops | bytes accessed | tf_op | source)
XLA Modules:
  0.0 110.3 jit_solution(11331195118409201033)
XLA Ops:
  0.0 0.0 copy-start
  0.0 1.4 %pad_convert_fusion.biases = f32[8,256]{1,0:T(8,128)} fusion(bf16[2,256]{1,0:T(2,128)(2,1)} %bitcast.15), kind=kLoop, calls=%fused_computation.2 | loop fusion | flops 2048 | bytes 9216 | tf_op jit(solution)/shard_map/jit(_pad)/pad | solution.py:480
  1.4 0.0 copy-done
  1.4 1.3 %copy_bitcast_fusion.1.states = bf16[2,8,192,256]{3,2,1,0:T(8,128)(2,1)} fusion(bf16[2,24,8,8,256]{4,3,2,1,0:T(8,128)(2,1)S(1)} %copy-done), kind=kLoop, calls=%fused_computation.1 | loop fusion | bytes 3145728 | tf_op jit(solution)/shard_map/reshape | solution.py:478
  2.7 104.8 %shard_map.64 = bf16[2,8,192,256]{3,2,1,0:T(8,128)(2,1)} custom-call(s32[8]{0:T(128)} %placement.1, s32[2560]{0:T(1024)} %constant.6.clone.table, bf16[2,8,192,256]{3,2,1,0:T(8,128)(2,1)} %copy_bitcast_fusion.1.states, bf16[2,3,768,256]{3,2,1,0:T(8,128)(2,1)} %bitcast.16, bf16[256,256]{1,0:T(8,128)(2,1)} %bitcast.17, f32[8,256]{1,0:T(8,128)} %pad_convert_fusion.biases), custom_call_target="tpu_custom_call" | custom-call | flops 7650410496 | bytes 16777216 | tf_op jit(solution)/shard_map/pallas_call | solution.py:487
  107.6 2.8 %copy_bitcast_fusion = bf16[1,2,24,8,8,256]{5,4,3,2,1,0:T(8,128)(2,1)} fusion(bf16[2,8,192,256]{3,2,1,0:T(8,128)(2,1)} %shard_map.64), kind=kLoop, calls=%fused_computation | loop fusion | bytes 3145728 | tf_op jit(solution)/shard_map/broadcast_in_dim | solution.py:526
Async XLA Ops:
  0.0 1.4 %copy-start = (bf16[2,24,8,8,256]{4,3,2,1,0:T(8,128)(2,1)S(1)}, bf16[2,24,8,8,256]{4,3,2,1,0:T(8,128)(2,1)}, u32[]{:S(2)}) copy-start(bf16[2,24,8,8,256]{4,3,2,1,0:T(8,128)(2,1)} %param.6) | copy-start | bytes 4718596
